TPU v7x, 32 devices: a whole 2x2x4 slice. The times are simulated.
32 devices in a mesh: cells: 8 (over z, x), seq: 4 (over y, core).
Axes of the slice: x: 2, y: 2, z: 4, core: 2. Of those that a mesh axis runs over, the one named last changes fastest.
Arguments:
- cell_tokens: bfloat16 [8, 1280, 1120], P('cells', 'seq'), may hold values from -6 to 6
- drop_counts: int32 [8], P('cells'), may hold values from 0 to 4, as said below
- lengths: int32 [8], P('cells'), may hold values from 640 to 1280, as said below
- ln_gain: bfloat16 [2, 1120], replicated, may hold values from 0.25 to 1.75
- ln_shift: bfloat16 [2, 1120], replicated, may hold values from -1.1953125 to 1.1953125
- w_qkv: bfloat16 [3, 1120, 1120], P(None, None, 'seq'), may hold values from -0.1875 to 0.1875
- qv_bias: bfloat16 [2, 1120], P(None, 'seq'), may hold values from -0.29882812 to 0.29882812
- w_out: bfloat16 [1120, 1120], P('seq'), may hold values from -1.5 to 1.5
- out_bias: bfloat16 [2, 1120], replicated, may hold values from -1.1953125 to 1.1953125
- w_up: bfloat16 [4480, 1120], P('cells', 'seq'), may hold values from -0.1875 to 0.1875
- up_bias: bfloat16 [4480], replicated, may hold values from -1.1953125 to 1.1953125
- w_down: bfloat16 [4480, 1120], P('cells', 'seq'), may hold values from -0.09375 to 0.09375
- out_grad: bfloat16 [8, 1280, 1120], P('cells', 'seq'), may hold values from -6 to 6
Outputs:
- block_out: bfloat16 [8, 1280, 1120], P('cells', 'seq')
- in_grad: float32 [8, 1280, 1120], P('cells', 'seq')
- d_ln_gain: float32 [2, 1120], replicated
- d_ln_shift: float32 [2, 1120], replicated
- d_qkv: float32 [3, 1120, 1120], P(None, None, 'seq')
- d_qv_bias: float32 [2, 1120], P(None, 'seq')
- d_out: float32 [1120, 1120], P('seq')
- d_out_bias: float32 [2, 1120], replicated
- d_up: float32 [4480, 1120], P('cells', 'seq')
- d_up_bias: float32 [4480], replicated
- d_down: float32 [4480, 1120], P('cells', 'seq')
Inputs may be any that keep to these rules, and one draw needn't show every extreme that they name: `drop_counts`: one sentence in every draw masks its first 4 positions as keys and one masks none. `lengths`: in every draw one sentence is 1280 long and one is 640 long.
All inputs are finite; a program needn't handle non-finite values.
Results may differ from a plain program's by a relative error of at most 0.012.
The roundings to bfloat16 on the way count: a program that leaves them out, or rounds other values in their place, can miss the bound.
Values may be sent and summed in bfloat16 or wider, within the bound.
A program may use at most 256 MiB of HBM per device.

v0:
```python
import math

import jax
import jax.numpy as jnp
from jax import lax
from jax.sharding import PartitionSpec as P

HEADS = 20
HD = 56
QBLOCK = 640


epsilon = 1e-05
masked_score = -1e30


def layer_norm(rows, gain, shift):
    centre = jnp.mean(rows, axis=-1, keepdims=True)
    offsets = rows - centre
    spread = jnp.mean(offsets * offsets, axis=-1, keepdims=True)
    return offsets * lax.rsqrt(spread + epsilon) * gain + shift


def gelu_tanh(values):
    return jax.nn.gelu(values, approximate=True)


def visible(drop_counts, lengths, start_row, row_count, key_count):
    query_place = start_row + jnp.arange(row_count, dtype=jnp.int32)[:, None]
    key_place = jnp.arange(key_count, dtype=jnp.int32)[None, :]
    dropped = drop_counts[:, None, None, None]
    limits = lengths[:, None, None, None]
    return (
        (key_place <= query_place)
        & (key_place < limits)
        & ((key_place >= dropped) | (key_place == query_place))
    )


def attend(packed, drop_counts, lengths, scale):
    queries = packed[:, :, :, 0]
    keys_all = packed[:, :, :, 1]
    values = packed[:, :, :, 2]
    outputs = []
    log_sums = []
    for start_row in range(0, queries.shape[1], QBLOCK):
        end_row = start_row + QBLOCK
        scores = (
            jnp.einsum(
                "cqhe,ckhe->chqk",
                queries[:, start_row:end_row],
                keys_all[:, :end_row],
                preferred_element_type=jnp.float32,
            )
            * scale
        )
        allowed = visible(drop_counts, lengths, start_row, QBLOCK, end_row)
        scores = jnp.where(allowed, scores, masked_score)
        largest = jnp.max(scores, axis=-1, keepdims=True)
        weights = jnp.where(allowed, jnp.exp(scores - largest), 0.0)
        totals = jnp.sum(weights, axis=-1, keepdims=True)
        probs = (weights / totals).astype(jnp.bfloat16)
        piece_out = jnp.einsum(
            "chqk,ckhe->cqhe", probs, values[:, :end_row], preferred_element_type=jnp.float32
        )
        outputs.append(piece_out.astype(jnp.bfloat16))
        log_sums.append(jnp.transpose((largest + jnp.log(totals))[..., 0], (0, 2, 1)))
    return (jnp.concatenate(outputs, axis=1), jnp.concatenate(log_sums, axis=1))


def attend_back(packed, grad_out, log_sums, drop_counts, lengths, scale):
    queries = packed[:, :, :, 0]
    keys_all = packed[:, :, :, 1]
    values = packed[:, :, :, 2]
    grad_query = []
    grad_key = jnp.zeros(keys_all.shape, jnp.float32)
    grad_value = jnp.zeros(values.shape, jnp.float32)
    for start_row in range(0, queries.shape[1], QBLOCK):
        end_row = start_row + QBLOCK
        scores = (
            jnp.einsum(
                "cqhe,ckhe->chqk",
                queries[:, start_row:end_row],
                keys_all[:, :end_row],
                preferred_element_type=jnp.float32,
            )
            * scale
        )
        allowed = visible(drop_counts, lengths, start_row, QBLOCK, end_row)
        block_sums = jnp.transpose(log_sums[:, start_row:end_row], (0, 2, 1))[..., None]
        probs = jnp.where(
            allowed, jnp.exp(jnp.where(allowed, scores, masked_score) - block_sums), 0.0
        )
        grad_rows = grad_out[:, start_row:end_row]
        grad_probs = jnp.einsum(
            "cqhe,ckhe->chqk", grad_rows, values[:, :end_row], preferred_element_type=jnp.float32
        )
        centre = jnp.sum(probs * grad_probs, axis=-1, keepdims=True)
        grad_scores = (probs * (grad_probs - centre) * scale).astype(jnp.bfloat16)
        grad_query.append(
            jnp.einsum(
                "chqk,ckhe->cqhe",
                grad_scores,
                keys_all[:, :end_row],
                preferred_element_type=jnp.float32,
            ).astype(jnp.bfloat16)
        )
        grad_key = grad_key.at[:, :end_row].add(
            jnp.einsum(
                "chqk,cqhe->ckhe",
                grad_scores,
                queries[:, start_row:end_row],
                preferred_element_type=jnp.float32,
            )
        )
        grad_value = grad_value.at[:, :end_row].add(
            jnp.einsum(
                "chqk,cqhe->ckhe",
                probs.astype(jnp.bfloat16),
                grad_rows,
                preferred_element_type=jnp.float32,
            )
        )
    return jnp.stack(
        [
            jnp.concatenate(grad_query, axis=1),
            grad_key.astype(jnp.bfloat16),
            grad_value.astype(jnp.bfloat16),
        ],
        axis=3,
    )


def head_bias(pair_bias, head_count):
    stacked = jnp.stack([pair_bias[0], jnp.zeros_like(pair_bias[0]), pair_bias[1]]).astype(
        jnp.float32
    )
    return jnp.transpose(stacked.reshape(3, head_count, HD), (1, 0, 2))


def bias_grads(grad_packed):
    summed = jnp.sum(grad_packed, axis=(0, 1), dtype=jnp.float32)
    return jnp.stack([summed[:, 0].reshape(-1), summed[:, 2].reshape(-1)])


def body(
    cell_tokens,
    drop_counts,
    lengths,
    ln_gain,
    ln_shift,
    w_qkv,
    qv_bias,
    w_out,
    out_bias,
    w_up,
    up_bias,
    w_down,
    out_grad,
):
    scale = 1.0 / math.sqrt(HD)
    up_rows, down_rows = (
        lax.all_gather(w_up, "cells", axis=0, tiled=True),
        lax.all_gather(w_down, "cells", axis=0, tiled=True),
    )
    up_unit, down_unit = (
        lax.all_to_all(up_rows, "seq", split_axis=0, concat_axis=1, tiled=True),
        lax.all_to_all(down_rows, "seq", split_axis=0, concat_axis=1, tiled=True),
    )
    gains = ln_gain.astype(jnp.float32)
    shifts = ln_shift.astype(jnp.float32)
    biases = out_bias.astype(jnp.float32)
    tokens = cell_tokens.astype(jnp.float32)
    cells_here, rows_here, width = tokens.shape
    normed_f, norm_back = jax.vjp(layer_norm, tokens, gains[0], shifts[0])
    normed = normed_f.astype(jnp.bfloat16)
    qkv_full, out_full, bias_full = (
        lax.all_gather(w_qkv, "seq", axis=2, tiled=True),
        lax.all_gather(w_out, "seq", axis=0, tiled=True),
        lax.all_gather(qv_bias, "seq", axis=1, tiled=True),
    )
    qkv_heads = qkv_full.reshape(3, width, HEADS, HD)
    packed = jnp.einsum(
        "csd,tdhe->cshte", normed, qkv_heads, preferred_element_type=jnp.float32
    ) + head_bias(bias_full, HEADS)
    packed = packed.astype(jnp.bfloat16)
    group_count = lax.axis_size("seq")
    grouped = packed.reshape(cells_here, rows_here, group_count, HEADS // group_count, 3, HD)
    moved_heads = lax.all_to_all(grouped, "seq", split_axis=2, concat_axis=1, tiled=True)[:, :, 0]
    head_out, log_sums = attend(moved_heads, drop_counts, lengths, scale)
    head_out, log_sums, moved_kept = (head_out, log_sums, moved_heads)
    mixed = lax.all_to_all(head_out, "seq", split_axis=1, concat_axis=2, tiled=True).reshape(
        cells_here, rows_here, width
    )
    branch = (
        jnp.einsum("csd,de->cse", mixed, out_full, preferred_element_type=jnp.float32) + biases[0]
    )
    middle = tokens + branch
    normed2_f, norm_back2 = jax.vjp(layer_norm, middle, gains[1], shifts[1])
    normed2 = normed2_f.astype(jnp.bfloat16)
    normed2_all, grad_all = (
        lax.all_gather(normed2, "seq", axis=1, tiled=True),
        lax.all_gather(out_grad, "seq", axis=1, tiled=True),
    )
    units = up_unit.shape[0]
    first_unit = lax.axis_index("seq") * units
    bias_unit = lax.dynamic_slice_in_dim(up_bias, first_unit, units).astype(jnp.float32)
    hidden = (
        jnp.einsum("csd,fd->csf", normed2_all, up_unit, preferred_element_type=jnp.float32)
        + bias_unit
    )
    active_f, gelu_back = jax.vjp(gelu_tanh, hidden)
    active = active_f.astype(jnp.bfloat16)
    down_terms = jnp.einsum("csf,fd->csd", active, down_unit, preferred_element_type=jnp.float32)
    branch2 = (
        lax.psum_scatter(
            down_terms.astype(jnp.bfloat16), "seq", scatter_dimension=1, tiled=True
        ).astype(jnp.float32)
        + biases[1]
    )
    block_out = (middle + branch2).astype(jnp.bfloat16)
    grad_down_unit = jnp.einsum("csf,csd->fd", active, grad_all, preferred_element_type=jnp.float32)
    grad_active = jnp.einsum("csd,fd->csf", grad_all, down_unit, preferred_element_type=jnp.float32)
    grad_hidden = gelu_back(grad_active)[0].astype(jnp.bfloat16)
    grad_up_unit = jnp.einsum(
        "csf,csd->fd", grad_hidden, normed2_all, preferred_element_type=jnp.float32
    )
    unit_bias_grad = jnp.sum(grad_hidden, axis=(0, 1), dtype=jnp.float32)
    grad_up_bias = lax.dynamic_update_slice_in_dim(
        jnp.zeros((up_bias.shape[0],), jnp.float32), unit_bias_grad, first_unit, 0
    )
    normed2_terms = jnp.einsum(
        "csf,fd->csd", grad_hidden, up_unit, preferred_element_type=jnp.float32
    )
    grad_normed2 = lax.psum_scatter(normed2_terms, "seq", scatter_dimension=1, tiled=True)
    up_part, down_part = (
        lax.all_to_all(grad_up_unit, "seq", split_axis=1, concat_axis=0, tiled=True),
        lax.all_to_all(grad_down_unit, "seq", split_axis=1, concat_axis=0, tiled=True),
    )
    grad_middle_norm, grad_gain2, grad_shift2 = norm_back2(grad_normed2)
    grad_middle = out_grad.astype(jnp.float32) + grad_middle_norm
    grad_branch = grad_middle.astype(jnp.bfloat16)
    grad_bias_attn = jnp.sum(grad_branch, axis=(0, 1), dtype=jnp.float32)
    grad_bias_down = jnp.sum(out_grad, axis=(0, 1), dtype=jnp.float32)
    d_up, d_down = (
        lax.psum_scatter(up_part, "cells", scatter_dimension=0, tiled=True),
        lax.psum_scatter(down_part, "cells", scatter_dimension=0, tiled=True),
    )
    grad_out_w = jnp.einsum("csd,cse->de", mixed, grad_branch, preferred_element_type=jnp.float32)
    grad_mixed = jnp.einsum(
        "cse,de->csd", grad_branch, out_full, preferred_element_type=jnp.float32
    ).astype(jnp.bfloat16)
    grad_mixed = grad_mixed.reshape(cells_here, rows_here, HEADS, HD)
    grad_heads = lax.all_to_all(grad_mixed, "seq", split_axis=2, concat_axis=1, tiled=True)
    grad_packed_heads = attend_back(moved_kept, grad_heads, log_sums, drop_counts, lengths, scale)
    grad_packed = lax.all_to_all(grad_packed_heads, "seq", split_axis=1, concat_axis=2, tiled=True)
    grad_qkv_full = jnp.einsum(
        "csd,cshte->tdhe", normed, grad_packed, preferred_element_type=jnp.float32
    ).reshape(3, width, width)
    grad_normed = jnp.einsum(
        "cshte,tdhe->csd", grad_packed, qkv_heads, preferred_element_type=jnp.float32
    )
    grad_qkv_own, grad_bias_own, grad_out_own = (
        lax.psum_scatter(grad_qkv_full, "seq", scatter_dimension=2, tiled=True),
        lax.psum_scatter(bias_grads(grad_packed), "seq", scatter_dimension=1, tiled=True),
        lax.psum_scatter(grad_out_w, "seq", scatter_dimension=0, tiled=True),
    )
    d_qkv, d_qv_bias, d_out = lax.psum((grad_qkv_own, grad_bias_own, grad_out_own), "cells")
    grad_tokens_norm, grad_gain1, grad_shift1 = norm_back(grad_normed)
    in_grad = grad_middle + grad_tokens_norm
    d_ln_gain, d_ln_shift, d_out_bias, d_up_bias = lax.psum(
        (
            jnp.stack([grad_gain1, grad_gain2]),
            jnp.stack([grad_shift1, grad_shift2]),
            jnp.stack([grad_bias_attn, grad_bias_down]),
            grad_up_bias,
        ),
        ("cells", "seq"),
    )
    return (
        block_out,
        in_grad,
        d_ln_gain,
        d_ln_shift,
        d_qkv,
        d_qv_bias,
        d_out,
        d_out_bias,
        d_up,
        d_up_bias,
        d_down,
    )


def solution(mesh):
    placed = (
        P("cells", "seq", None),
        P("cells"),
        P("cells"),
        P(),
        P(),
        P(None, None, "seq"),
        P(None, "seq"),
        P("seq", None),
        P(),
        P("cells", "seq"),
        P(),
        P("cells", "seq"),
        P("cells", "seq", None),
    )
    return jax.shard_map(
        body,
        mesh=mesh,
        in_specs=placed,
        out_specs=(
            P("cells", "seq", None),
            P("cells", "seq", None),
            P(),
            P(),
            P(None, None, "seq"),
            P(None, "seq"),
            P("seq", None),
            P(),
            P("cells", "seq"),
            P(),
            P("cells", "seq"),
        ),
        check_vma=False,
    )
```

profile of v0, /device:TPU:0, one launch (start us, length us, event | category | flops | bytes accessed | tf_op | source)
XLA Modules:
  0.0 1320.8 jit_solution(9016403108067090573)
XLA Ops:
  21.2 45.7 %all-gather.10.cloned.1.call-done = bf16[3,1120,1120]{1,2,0:T(8,128)(2,1)} async-done(((bf16[3,1120,280]{1,2,0:T(8,128)(2,1)}), bf16[3,1120,1120]{1,2,0:T(8,128)(2,1)}) %all-gather.10.cloned.1.call-update) | async-done | bytes 7526416 | tf_op jit(solution)/shard_map/all_gather | solution.py:178
  84.5 35.4 %all-to-all-done = bf16[1,320,4,5,3,56]{1,5,3,4,0,2:T(8,128)(2,1)S(1)} async-done(((bf16[1,320,4,5,3,56]{1,5,3,4,0,2:T(8,128)(2,1)}), bf16[1,320,4,5,3,56]{1,5,3,4,0,2:T(8,128)(2,1)S(1)}, u32[]{:S(2)}, u32[]{:S(2)}) %all-to-all-start) | async-done | bytes 2150432 | tf_op jit(solution)/shard_map/all_to_all | solution.py:189
  172.8 10.9 all-to-all-done.1
  234.2 25.7 %all-to-all-done.2 = bf16[4,1120,280]{1,2,0:T(8,128)(2,1)} async-done(((bf16[4,1120,280]{1,2,0:T(8,128)(2,1)}), bf16[4,1120,280]{1,2,0:T(8,128)(2,1)}, u32[]{:S(2)}, u32[]{:S(2)}) %all-to-all-start.2) | async-done | bytes 2508832 | tf_op jit(solution)/shard_map/all_to_all | solution.py:167
  274.4 33.1 %all-gather.16.cloned.1.call-done = bf16[1,1280,1120]{2,1,0:T(8,128)(2,1)} async-done(((bf16[1,320,1120]{2,1,0:T(8,128)(2,1)}), bf16[1,1280,1120]{2,1,0:T(8,128)(2,1)}) %all-gather.16.cloned.1.call-update) | async-done | bytes 2867216 | tf_op jit(solution)/shard_map/all_gather | solution.py:203
  311.2 12.6 convert_reduce_fusion
  343.9 45.1 %reduce-scatter.16.cloned.1.call-done = f32[1,320,1120]{2,1,0:T(8,128)} async-done(((f32[1,1280,1120]{2,1,0:T(8,128)}), f32[1,320,1120]{2,1,0:T(8,128)}) %reduce-scatter.16.cloned.1.call-update) | async-done | bytes 1433616 | tf_op jit(solution)/shard_map/reduce_scatter | solution.py:235
  391.0 38.1 %reduce-scatter.14.cloned.1.call-done = bf16[1,320,1120]{2,1,0:T(8,128)(2,1)} async-done(((bf16[1,1280,1120]{2,1,0:T(8,128)(2,1)}), bf16[1,320,1120]{2,1,0:T(8,128)(2,1)}) %reduce-scatter.14.cloned.1.call-update) | async-done | bytes 716816 | tf_op jit(solution)/shard_map/reduce_scatter | solution.py:216
  445.8 11.9 all-to-all-done.4
  464.5 17.3 %fusion.123 = bf16[1,640,5,56]{1,3,2,0:T(8,128)(2,1)} fusion(f32[5,640,640]{1,2,0:T(8,128)} %fusion.146, bf16[1,1280,5,56]{1,3,2,0:T(8,128)(2,1)S(1)} %copy-done.19, f32[5,640,640]{1,2,0:T(8,128)} %copy-done.7, f32[5,640]{1,0:T(8,128)S(1)} %log_add_fusion.1, pred[640,640]{0,1:T(8,128)(4,1)S(1)} %copy-done.14), kind=kOutput, calls=%fused_computation.124 | convolution fusion | flops 256183040 | bytes 34344960 | tf_op jit(solution)/shard_map/chqk,ckhe->cqhe/dot_general | solution.py:101
  481.7 17.6 %fusion.111 = f32[1,640,5,56]{1,3,2,0:T(8,128)} fusion(f32[5,640,640]{1,2,0:T(8,128)} %fusion.146, bf16[1,1280,5,56]{1,3,2,0:T(8,128)(2,1)} %copy-done.15, f32[5,640,640]{1,2,0:T(8,128)} %copy-done.7, f32[5,640]{1,0:T(8,128)S(1)} %log_add_fusion.1, pred[640,640]{0,1:T(8,128)(4,1)S(1)} %copy-done.14), kind=kOutput, calls=%fused_computation.118 | convolution fusion | flops 256003840 | bytes 34703360 | tf_op jit(solution)/shard_map/chqk,cqhe->ckhe/dot_general | solution.py:109
  508.3 35.1 %fusion.91 = bf16[1,1280,5,1,56]{1,4,2,3,0:T(8,128)(2,1)} fusion(f32[5,640,1280]{2,1,0:T(8,128)} %fusion.139, f32[5,640,1280]{2,1,0:T(8,128)} %get-tuple-element.107, f32[5,640]{1,0:T(8,128)S(1)} %log_add_fusion, pred[640,1280]{1,0:T(8,128)(4,1)} %fusion.57, f32[1,640,5,56]{1,3,2,0:T(8,128)} %fusion.111, bf16[1,1280,5,56]{1,3,2,0:T(8,128)(2,1)} %copy-done.15), kind=kOutput, calls=%fused_computation.84 | convolution fusion | flops 496337280 | bytes 69007360 | tf_op jit(solution)/shard_map/chqk,cqhe->ckhe/dot_general | solution.py:109
  543.4 33.6 %fusion.127 = bf16[1,640,5,56]{1,3,2,0:T(8,128)(2,1)} fusion(f32[5,640,1280]{2,1,0:T(8,128)} %fusion.139, f32[5,640,1280]{2,1,0:T(8,128)} %get-tuple-element.107, f32[5,640]{1,0:T(8,128)S(1)} %log_add_fusion, pred[640,1280]{1,0:T(8,128)(4,1)} %fusion.57, bf16[1,1280,5,3,56]{1,4,2,3,0:T(8,128)(2,1)S(1)} %copy-done.2), kind=kOutput, calls=%fused_computation.126 | convolution fusion | flops 495799680 | bytes 68290560 | tf_op jit(solution)/shard_map/chqk,ckhe->cqhe/dot_general | solution.py:101
  599.2 10.5 reshape.829
  609.8 29.5 %all_to_all.133 = bf16[4,2,134400]{2,1,0:T(2,128)(2,1)} all-to-all(bf16[4,2,134400]{2,1,0:T(2,128)(2,1)S(1)} %reshape.829), channel_id=1, replica_groups=mesh['cells'=8,'seq'=4] {'seq'}, dimensions={0} | all-to-all | bytes 4300800 | tf_op jit(solution)/shard_map/all_to_all | solution.py:256
  639.3 12.7 reshape.830
  652.0 11.0 copy.105
  673.2 11.8 copy.108
  699.2 104.3 %all_to_all.134 = f32[1120,4,280]{0,2,1:T(8,128)} all-to-all(f32[1120,4,280]{0,2,1:T(8,128)S(1)} %fusion.64), channel_id=1, replica_groups=mesh['cells'=8,'seq'=4] {'seq'}, dimensions={1} | all-to-all | bytes 10035200 | tf_op jit(solution)/shard_map/all_to_all | solution.py:238
  822.4 77.0 %all_to_all.135 = f32[1120,4,280]{0,2,1:T(8,128)} all-to-all(f32[1120,4,280]{0,2,1:T(8,128)S(1)} %fusion.66), channel_id=1, replica_groups=mesh['cells'=8,'seq'=4] {'seq'}, dimensions={1} | all-to-all | bytes 10035200 | tf_op jit(solution)/shard_map/all_to_all | solution.py:237
  929.0 22.6 %psum.52 = f32[2,280]{1,0:T(2,128)} all-reduce(f32[2,280]{1,0:T(2,128)S(1)} %constant_dynamic-slice_fusion), channel_id=1, replica_groups=mesh['cells'=8,'seq'=4] {'cells'}, use_global_device_ids=true, to_apply=%region_26.27 | all-reduce | flops 560 | bytes 4480 | tf_op jit(solution)/shard_map/psum | solution.py:268
  951.7 41.8 %all-reduce.4 = (f32[2,1120]{1,0:T(2,128)}, f32[2,1120]{1,0:T(2,128)}, f32[2,1120]{1,0:T(2,128)}, f32[4480]{0:T(1024)}) all-reduce(f32[2,1120]{1,0:T(2,128)S(1)} %pad_maximum_fusion.2, f32[2,1120]{1,0:T(2,128)S(1)} %pad_maximum_fusion.3, f32[2,1120]{1,0:T(2,128)S(1)} %pad_maximum_fusion.5, ...), channel_id=1, replica_groups=mesh['cells'=8,'seq'=4] {'cells','seq'}, use_global_device_ids=true, to_apply=%region_18.19 | all-reduce | flops 11200 | bytes 89600 | tf_op jit(solution)/shard_map/psum | solution.py:271
  995.9 127.5 %reduce-scatter.20.cloned.1.call-done = f32[560,280]{1,0:T(8,128)} async-done(((f32[4480,280]{1,0:T(8,128)}), f32[560,280]{1,0:T(8,128)}) %reduce-scatter.20.cloned.1.call-update) | async-done | bytes 627216
  1125.7 183.0 %all-reduce.8.cloned.1.call-done = (f32[3,1120,280]{1,2,0:T(8,128)}, f32[280,1120]{1,0:T(8,128)}) async-done(((f32[3,1120,280]{1,2,0:T(8,128)}, f32[280,1120]{1,0:T(8,128)}), (f32[3,1120,280]{1,2,0:T(8,128)}, f32[280,1120]{1,0:T(8,128)})) %all-reduce.8.cloned.1.call-update) | async-done | bytes 5017616 | tf_op jit(solution)/shard_map/psum | solution.py:268
  (221 shorter events, 310.0 us)
Async XLA Ops:
  7.2 59.7 %all-gather.10.cloned.1.call-start = ((), (), s32[]{:S(2)}) async-start(), calls=%async_computation.14 | async-start | bytes 9676800 | tf_op jit(solution)/shard_map/all_gather | solution.py:178
  7.9 183.0 %all-gather.12.cloned.1.call-start = ((), (), s32[]{:S(2)}) async-start(), calls=%async_computation.15 | async-start | bytes 3225600 | tf_op jit(solution)/shard_map/all_gather | solution.py:179
  8.7 188.1 %all-gather.18.cloned.1.call-start = ((), (), s32[]{:S(2)}) async-start(), calls=%async_computation.21 | async-start | bytes 3225600 | tf_op jit(solution)/shard_map/all_gather | solution.py:163
  17.5 56.8 %copy-start.21 = (f32[1120]{0:T(1024)}, f32[1120]{0:T(1024)S(1)}, u32[]{:S(2)}) copy-start(f32[1120]{0:T(1024)S(1)} %get-tuple-element.85) | copy-start | bytes 13444
  17.6 56.8 %copy-start.27 = (f32[1120]{0:T(1024)}, f32[1120]{0:T(1024)S(1)}, u32[]{:S(2)}) copy-start(f32[1120]{0:T(1024)S(1)} %get-tuple-element.87) | copy-start | bytes 13444
  19.0 55.4 %copy-start.23 = (f32[320]{0:T(512)}, f32[320]{0:T(512)S(1)}, u32[]{:S(2)}) copy-start(f32[320]{0:T(512)S(1)} %broadcast_multiply_fusion.1) | copy-start | bytes 3844
  21.2 53.2 %copy-start.25 = (f32[320]{0:T(512)}, f32[320]{0:T(512)S(1)}, u32[]{:S(2)}) copy-start(f32[320]{0:T(512)S(1)} %fusion.148) | copy-start | bytes 3844
  76.8 43.2 %all-to-all-start = ((bf16[1,320,4,5,3,56]{1,5,3,4,0,2:T(8,128)(2,1)}), bf16[1,320,4,5,3,56]{1,5,3,4,0,2:T(8,128)(2,1)S(1)}, u32[]{:S(2)}, u32[]{:S(2)}) async-start(bf16[1,320,4,5,3,56]{1,5,3,4,0,2:T(8,128)(2,1)} %copy.87), calls=%async_computation | async-start | bytes 5160960 | tf_op jit(solution)/shard_map/all_to_all | solution.py:189
  80.4 140.4 %all-gather.20.cloned.1.call-start = ((), (), s32[]{:S(2)}) async-start(), calls=%async_computation.22 | async-start | bytes 3225600 | tf_op jit(solution)/shard_map/all_gather | solution.py:164
  82.6 57.5 %copy-start.13 = (pred[640,640]{0,1:T(8,128)(4,1)}, pred[640,640]{0,1:T(8,128)(4,1)S(1)}, u32[]{:S(2)}) copy-start(pred[640,640]{0,1:T(8,128)(4,1)S(1)} %fusion.101) | copy-start | bytes 1228804
  168.5 15.2 %all-to-all-start.1 = ((bf16[4,2,44800]{2,1,0:T(2,128)(2,1)}), bf16[4,2,44800]{2,1,0:T(2,128)(2,1)}, u32[]{:S(2)}, u32[]{:S(2)}) async-start(bf16[4,2,44800]{2,1,0:T(2,128)(2,1)} %reshape.827), calls=%async_computation.1 | async-start | bytes 1433600 | tf_op jit(solution)/shard_map/all_to_all | solution.py:192
  172.7 92.6 %all-gather.14.cloned.1.call-start = ((), (), s32[]{:S(2)}) async-start(), calls=%async_computation.16 | async-start | bytes 3686400 | tf_op jit(solution)/shard_map/all_gather | solution.py:202
  196.2 111.3 %all-gather.16.cloned.1.call-start = ((), (), s32[]{:S(2)}) async-start(), calls=%async_computation.18 | async-start | bytes 3686400 | tf_op jit(solution)/shard_map/all_gather | solution.py:203
  210.1 49.8 %all-to-all-start.2 = ((bf16[4,1120,280]{1,2,0:T(8,128)(2,1)}), bf16[4,1120,280]{1,2,0:T(8,128)(2,1)}, u32[]{:S(2)}, u32[]{:S(2)}) async-start(bf16[4,1120,280]{1,2,0:T(8,128)(2,1)} %copy.93), calls=%async_computation.2 | async-start | bytes 5160960 | tf_op jit(solution)/shard_map/all_to_all | solution.py:167
  259.9 51.3 %all-to-all-start.3 = ((bf16[4,1120,280]{1,2,0:T(8,128)(2,1)}), bf16[4,1120,280]{1,2,0:T(8,128)(2,1)}, u32[]{:S(2)}, u32[]{:S(2)}) async-start(bf16[4,1120,280]{1,2,0:T(8,128)(2,1)} %copy.95), calls=%async_computation.3 | async-start | bytes 5160960 | tf_op jit(solution)/shard_map/all_to_all | solution.py:168
  264.5 124.6 %reduce-scatter.16.cloned.1.call-start = ((), (), s32[]{:S(2)}) async-start(), calls=%async_computation.19 | async-start | bytes 7372800 | tf_op jit(solution)/shard_map/reduce_scatter | solution.py:235
  333.4 95.7 %reduce-scatter.14.cloned.1.call-start = ((), (), s32[]{:S(2)}) async-start(), calls=%async_computation.17 | async-start | bytes 3686400 | tf_op jit(solution)/shard_map/reduce_scatter | solution.py:216
  343.9 562.4 %reduce-scatter.24.cloned.1.call-start = ((), (), s32[]{:S(2)}) async-start(), calls=%async_computation.25 | async-start | bytes 6451200
  391.0 42.6 %copy-start.6 = (bf16[1,4,320,5,56]{2,4,3,1,0:T(8,128)(2,1)S(1)}, bf16[1,4,320,5,56]{2,4,3,1,0:T(8,128)(2,1)}, u32[]{:S(2)}) copy-start(bf16[1,4,320,5,56]{2,4,3,1,0:T(8,128)(2,1)} %copy.91) | copy-start | bytes 2150404
  441.8 15.9 %all-to-all-start.4 = ((bf16[1,320,20,56]{1,3,0,2:T(8,128)(2,1)}), bf16[1,320,20,56]{1,3,0,2:T(8,128)(2,1)S(1)}, u32[]{:S(2)}, u32[]{:S(2)}) async-start(bf16[1,320,20,56]{1,3,0,2:T(8,128)(2,1)} %bitcast.48), calls=%async_computation.6 | async-start | bytes 1720320 | tf_op jit(solution)/shard_map/all_to_all | solution.py:254
  445.3 460.9 %reduce-scatter.18.cloned.1.call-start = ((), (), s32[]{:S(2)}) async-start(), calls=%async_computation.20 | async-start | bytes 19353600 | tf_op jit(solution)/shard_map/reduce_scatter | solution.py:264
  685.1 308.5 %reduce-scatter.22.cloned.1.call-start = ((), (), s32[]{:S(2)}) async-start(), calls=%async_computation.24 | async-start | bytes 7741440
  810.3 313.0 %reduce-scatter.20.cloned.1.call-start = ((), (), s32[]{:S(2)}) async-start(), calls=%async_computation.23 | async-start | bytes 7741440
  906.1 402.5 %all-reduce.8.cloned.1.call-start = ((), (), s32[]{:S(2)}) async-start(), calls=%async_computation.26 | async-start | bytes 10321920 | tf_op jit(solution)/shard_map/psum | solution.py:268
  (29 other events, 247.2 us)
Sparse Core Ops, SparseCore 0:
  9.6 57.3 all-gather.9
  68.5 34.0 all-gather.11
  104.8 57.7 all-gather.17
  164.7 56.1 all-gather.19
  222.8 39.9 all-gather.13
  264.2 43.1 all-gather.15
  333.5 55.4 reduce-scatter.15
  392.3 36.7 reduce-scatter.13
  437.6 50.8 reduce-scatter.23
  685.2 175.8 reduce-scatter.17
  865.2 128.2 reduce-scatter.21
  997.5 125.7 reduce-scatter.19
  1127.5 181.1 all-reduce.7
where the time goes:
time: 1330 us; the launch traced here: 1320 us
  waiting for transfers between devices  570 us (43%)
  blocking collectives  288 us (22%)
  matrix products  244 us (18%)
  local copies, waits for them, and re-layouts  147 us (11%)
  other arithmetic  33 us (2%)
  starting transfers between devices  22 us (2%)
  between operations  16.8 us (1%)
    psum x1, waiting for transfers between devices, body(): lax.psum((grad_qkv_own, grad_bias_own, grad_out_own), 'cells')  183 us
    unnamed x16, waiting for transfers between devices  131 us
    all_to_all x1, blocking collectives, body(): lax.all_to_all(grad_down_unit, 'seq', split_axis=1, concat_axis=0, tiled=...  104 us
    all_to_all x1, blocking collectives, body(): lax.all_to_all(grad_up_unit, 'seq', split_axis=1, concat_axis=0, tiled=True)  77 us
    unnamed x83, local copies, waits for them, and re-layouts  60.8 us
    dot_general x2, matrix products, attend_back(): jnp.einsum('chqk,cqhe->ckhe', grad_scores, queries[:, start_row:end_row],...  52.6 us
    dot_general x2, matrix products, attend_back(): jnp.einsum('chqk,ckhe->cqhe', grad_scores, keys_all[:, :end_row], preferr...  50.9 us
    all_gather x1, waiting for transfers between devices, body(): lax.all_gather(w_qkv, 'seq', axis=2, tiled=True)  45.7 us
  transfers between devices with their start and end apart: 18, of which 12 were waited for; matrix products, arithmetic and copies ran while one was open for 28% of the time, Pallas kernels for 0%

commit v1 on v0

v1 whole, which is shorter than its diff:
```python
import functools
import math

import jax
import jax.numpy as jnp
from jax import lax
from jax.experimental import pallas as pl
from jax.experimental.pallas import tpu as pltpu
from jax.sharding import PartitionSpec as P

HEADS = 20
HD = 56
LANES = 128
epsilon = 1e-05
masked = -1e30
BF = jnp.bfloat16
F32 = jnp.float32
VMEM_LIMIT = 60 * 1024 * 1024


def dot_nn(a, b):
    return lax.dot_general(a, b, (((1,), (0,)), ((), ())), preferred_element_type=F32)


def dot_nt(a, b):
    return lax.dot_general(a, b, (((1,), (1,)), ((), ())), preferred_element_type=F32)


def dot_tn(a, b):
    return lax.dot_general(a, b, (((0,), (0,)), ((), ())), preferred_element_type=F32)


def layer_norm(rows, gain, shift):
    centre = jnp.mean(rows, axis=-1, keepdims=True)
    offsets = rows - centre
    spread = jnp.mean(offsets * offsets, axis=-1, keepdims=True)
    return offsets * lax.rsqrt(spread + epsilon) * gain + shift


def gelu_tanh(values):
    return jax.nn.gelu(values, approximate=True)


def block_size(length):
    return 256 if length % 256 == 0 else length


def attend_kernel(drop_ref, len_ref, packed_ref, out_ref, lse_ref, q_sc, k_sc, v_sc, o_sc):
    heads, length, _ = q_sc.shape
    block = block_size(length)
    factor = (1.0 / math.sqrt(HD)) * math.log2(math.e)
    dropped, limit = drop_ref[0], len_ref[0]
    for t, sc in enumerate((q_sc, k_sc, v_sc)):
        sc[...] = jnp.zeros_like(sc)
        for h in range(heads):
            sc[h, :, :HD] = packed_ref[t, :, h * HD : (h + 1) * HD]
    key = lax.broadcasted_iota(jnp.int32, (1, length), 1)
    bias = jnp.where((key >= dropped) & (key < limit), 0.0, masked)

    def head(h, carry):
        for i in range(length // block):
            width = (i + 1) * block
            q = q_sc[h, pl.ds(i * block, block), :]
            raw = dot_nt(q, k_sc[h, pl.ds(0, width), :])
            row = i * block + lax.broadcasted_iota(jnp.int32, (block, block), 0)
            col = i * block + lax.broadcasted_iota(jnp.int32, (block, block), 1)
            ok = (col <= row) & (col < limit)
            if i == 0:
                ok = ok & ((col >= dropped) | (col == row))
            last = jnp.where(ok, raw[:, i * block :], masked)
            if i:
                raw = jnp.concatenate([raw[:, : i * block] + bias[:, : i * block], last], axis=1)
            else:
                raw = last
            top = jnp.max(raw, axis=1, keepdims=True) * factor
            weights = jnp.exp2(raw * factor - top)
            total = jnp.sum(weights, axis=1, keepdims=True)
            probs = (weights * (1.0 / total)).astype(BF)
            out = dot_nn(probs, v_sc[h, pl.ds(0, width), :])
            o_sc[h, pl.ds(i * block, block), :] = out.astype(BF)
            stat = jnp.broadcast_to(top + jnp.log2(total), (block, LANES))
            lse_ref[h, 0:1, pl.ds(i * block, block)] = jnp.transpose(stat)[0:1, :]
        return carry

    lax.fori_loop(0, heads, head, 0)
    for h in range(heads):
        out_ref[:, h * HD : (h + 1) * HD] = o_sc[h, :, :HD]


def attend(packed, drop_counts, lengths):
    _, length, width = packed.shape
    heads = width // HD
    return pl.pallas_call(
        attend_kernel,
        name="attend",
        out_shape=(
            jax.ShapeDtypeStruct((length, width), BF),
            jax.ShapeDtypeStruct((heads, 1, length), F32),
        ),
        in_specs=[
            pl.BlockSpec(memory_space=pltpu.SMEM),
            pl.BlockSpec(memory_space=pltpu.SMEM),
            pl.BlockSpec(memory_space=pltpu.VMEM),
        ],
        out_specs=(
            pl.BlockSpec(memory_space=pltpu.VMEM),
            pl.BlockSpec(memory_space=pltpu.VMEM),
        ),
        scratch_shapes=[pltpu.VMEM((heads, length, LANES), BF)] * 4,
        compiler_params=pltpu.CompilerParams(vmem_limit_bytes=VMEM_LIMIT),
    )(drop_counts, lengths, packed)


def attend_back_kernel(
    drop_ref, len_ref, packed_ref, out_ref, lse_ref, gout_ref, gpacked_ref,
    q_sc, k_sc, v_sc, g_sc, delta_sc, dq_sc, dk_sc, dv_sc,
):
    heads, length, _ = q_sc.shape
    block = block_size(length)
    scale = 1.0 / math.sqrt(HD)
    factor = scale * math.log2(math.e)
    dropped, limit = drop_ref[0], len_ref[0]
    for t, sc in enumerate((q_sc, k_sc, v_sc)):
        sc[...] = jnp.zeros_like(sc)
        for h in range(heads):
            sc[h, :, :HD] = packed_ref[t, :, h * HD : (h + 1) * HD]
    g_sc[...] = jnp.zeros_like(g_sc)
    for h in range(heads):
        part = slice(h * HD, (h + 1) * HD)
        g = gout_ref[:, part]
        g_sc[h, :, :HD] = g
        prod = jnp.sum(g.astype(F32) * out_ref[:, part].astype(F32), axis=1, keepdims=True)
        delta_sc[h, 0:1, :] = jnp.transpose(jnp.broadcast_to(prod, (length, LANES)))[0:1, :]
    key = lax.broadcasted_iota(jnp.int32, (length, 1), 0)
    bias = jnp.where((key >= dropped) & (key < limit), 0.0, masked)

    def head(h, carry):
        dq_sc[h] = jnp.zeros((length, LANES), F32)
        for j in range(length // block):
            low = j * block
            rest = length - low
            k = k_sc[h, pl.ds(low, block), :]
            v = v_sc[h, pl.ds(low, block), :]
            q = q_sc[h, pl.ds(low, rest), :]
            g = g_sc[h, pl.ds(low, rest), :]
            raw = dot_nt(k, q) * factor
            row = low + lax.broadcasted_iota(jnp.int32, (block, block), 1)
            col = low + lax.broadcasted_iota(jnp.int32, (block, block), 0)
            ok = (col <= row) & (col < limit)
            if j == 0:
                ok = ok & ((col >= dropped) | (col == row))
            first = jnp.where(ok, raw[:, :block], masked)
            if rest > block:
                raw = jnp.concatenate([first, raw[:, block:] + bias[low : low + block]], axis=1)
            else:
                raw = first
            probs = jnp.exp2(raw - lse_ref[h, 0:1, pl.ds(low, rest)])
            gprobs = dot_nt(v, g)
            gscores = (probs * (gprobs - delta_sc[h, 0:1, pl.ds(low, rest)])).astype(BF)
            dv_sc[h, pl.ds(low, block), :] = dot_nn(probs.astype(BF), g).astype(BF)
            dk_sc[h, pl.ds(low, block), :] = (dot_nn(gscores, q) * scale).astype(BF)
            dq_sc[h, pl.ds(low, rest), :] += dot_tn(gscores, k)
        return carry

    lax.fori_loop(0, heads, head, 0)
    for h in range(heads):
        part = slice(h * HD, (h + 1) * HD)
        gpacked_ref[0, :, part] = (dq_sc[h, :, :HD] * scale).astype(BF)
        gpacked_ref[1, :, part] = dk_sc[h, :, :HD]
        gpacked_ref[2, :, part] = dv_sc[h, :, :HD]


def attend_back(packed, attended, lse, grad_out, drop_counts, lengths):
    _, length, width = packed.shape
    heads = width // HD
    vmem = pl.BlockSpec(memory_space=pltpu.VMEM)
    smem = pl.BlockSpec(memory_space=pltpu.SMEM)
    return pl.pallas_call(
        attend_back_kernel,
        name="attend_back",
        out_shape=jax.ShapeDtypeStruct((3, length, width), BF),
        in_specs=[smem, smem, vmem, vmem, vmem, vmem],
        out_specs=vmem,
        scratch_shapes=[pltpu.VMEM((heads, length, LANES), BF)] * 4
        + [pltpu.VMEM((heads, 1, length), F32)]
        + [pltpu.VMEM((heads, length, LANES), F32)]
        + [pltpu.VMEM((heads, length, LANES), BF)] * 2,
        compiler_params=pltpu.CompilerParams(vmem_limit_bytes=VMEM_LIMIT),
    )(drop_counts, lengths, packed, attended, lse, grad_out)


def body(
    cell_tokens, drop_counts, lengths, ln_gain, ln_shift, w_qkv, qv_bias, w_out, out_bias,
    w_up, up_bias, w_down, out_grad,
):
    group = lax.axis_size("seq")
    cells = lax.axis_size("cells")
    place = lax.axis_index("seq")
    unit_rows, part_width = w_up.shape
    _, rows, width = cell_tokens.shape
    share = -(-unit_rows // (group * 16)) * 16
    full = group * share

    def split_units(w):
        padded = jnp.pad(w, ((0, full - unit_rows), (0, 0))).reshape(group, share, part_width)
        return padded

    both = jnp.stack([split_units(w_up), split_units(w_down)], axis=1)
    moved = lax.all_to_all(both, "seq", split_axis=0, concat_axis=0, tiled=True)
    mine = jnp.transpose(moved, (1, 2, 0, 3)).reshape(2, share, width)
    up_unit = lax.all_gather(mine[0], "cells", axis=0, tiled=True)
    down_unit = lax.all_gather(mine[1], "cells", axis=0, tiled=True)
    bias_rows = jnp.pad(
        up_bias.astype(F32).reshape(cells, unit_rows), ((0, 0), (0, full - unit_rows))
    ).reshape(cells, group, share)
    bias_unit = lax.dynamic_index_in_dim(bias_rows, place, 1, keepdims=False).reshape(-1)

    gains = ln_gain.astype(F32)
    shifts = ln_shift.astype(F32)
    biases = out_bias.astype(F32)
    tokens = cell_tokens[0].astype(F32)
    cot = out_grad[0]
    normed_f, norm_back = jax.vjp(layer_norm, tokens, gains[0], shifts[0])
    normed = normed_f.astype(BF)
    normed_all = lax.all_gather(normed, "seq", axis=0, tiled=True)
    head_bias = jnp.stack([qv_bias[0], jnp.zeros_like(qv_bias[0]), qv_bias[1]]).astype(F32)
    packed = (
        jnp.einsum("sd,tde->tse", normed_all, w_qkv, preferred_element_type=F32)
        + head_bias[:, None, :]
    ).astype(BF)
    attended, lse = attend(packed, drop_counts, lengths)
    branch_terms = dot_nn(attended, w_out).astype(BF)
    branch = lax.psum_scatter(branch_terms, "seq", scatter_dimension=0, tiled=True)
    middle = tokens + (branch.astype(F32) + biases[0])
    normed2_f, norm_back2 = jax.vjp(layer_norm, middle, gains[1], shifts[1])
    normed2 = normed2_f.astype(BF)
    normed2_all = lax.all_gather(normed2, "seq", axis=0, tiled=True)
    cot_all = lax.all_gather(cot, "seq", axis=0, tiled=True)
    hidden = dot_nt(normed2_all, up_unit) + bias_unit
    active_f, gelu_back = jax.vjp(gelu_tanh, hidden)
    active = active_f.astype(BF)
    down_terms = dot_nn(active, down_unit).astype(BF)
    grad_active = dot_nt(cot_all, down_unit)
    grad_hidden = gelu_back(grad_active)[0].astype(BF)
    normed2_terms = dot_nn(grad_hidden, up_unit).astype(BF)
    grad_normed2 = lax.psum_scatter(normed2_terms, "seq", scatter_dimension=0, tiled=True)
    branch2 = lax.psum_scatter(down_terms, "seq", scatter_dimension=0, tiled=True)
    block_out = (middle + (branch2.astype(F32) + biases[1])).astype(BF)
    grad_down_unit = dot_tn(active, cot_all).astype(BF)
    grad_up_unit = dot_tn(grad_hidden, normed2_all).astype(BF)
    unit_bias_grad = jnp.sum(grad_hidden, axis=0, dtype=F32).reshape(cells, share)
    placed_bias = lax.dynamic_update_index_in_dim(
        jnp.zeros((cells, group, share), F32), unit_bias_grad, place, 1
    )
    grad_up_bias = placed_bias.reshape(cells, full)[:, :unit_rows].reshape(-1)

    grad_middle_norm, grad_gain2, grad_shift2 = norm_back2(grad_normed2.astype(F32))
    grad_middle = cot.astype(F32) + grad_middle_norm
    grad_branch = grad_middle.astype(BF)
    grad_branch_all = lax.all_gather(grad_branch, "seq", axis=0, tiled=True)
    grad_bias_attn = jnp.sum(grad_branch, axis=0, dtype=F32)
    grad_bias_down = jnp.sum(cot, axis=0, dtype=F32)

    up_part = lax.psum_scatter(grad_up_unit, "cells", scatter_dimension=0, tiled=True)
    down_part = lax.psum_scatter(grad_down_unit, "cells", scatter_dimension=0, tiled=True)

    grad_out_own = dot_tn(attended, grad_branch_all)
    grad_heads = dot_nt(grad_branch_all, w_out).astype(BF)
    grad_packed = attend_back(packed, attended, lse, grad_heads, drop_counts, lengths)
    grad_qkv_own = jnp.einsum("sd,tse->tde", normed_all, grad_packed, preferred_element_type=F32)
    normed_terms = jnp.einsum("tse,tde->sd", grad_packed, w_qkv, preferred_element_type=F32)
    grad_normed = lax.psum_scatter(normed_terms.astype(BF), "seq", scatter_dimension=0, tiled=True)
    grad_bias_own = jnp.sum(grad_packed[::2], axis=1, dtype=F32)

    unit_parts = jnp.stack([up_part, down_part]).reshape(2, share, group, part_width)
    unit_parts = jnp.transpose(unit_parts, (2, 0, 1, 3))
    unit_moved = lax.all_to_all(unit_parts, "seq", split_axis=0, concat_axis=0, tiled=True)
    d_up = unit_moved[:, 0].reshape(full, part_width)[:unit_rows].astype(F32)
    d_down = unit_moved[:, 1].reshape(full, part_width)[:unit_rows].astype(F32)

    d_qkv, d_out = lax.psum((grad_qkv_own.astype(BF), grad_out_own.astype(BF)), "cells")
    grad_tokens_norm, grad_gain1, grad_shift1 = norm_back(grad_normed.astype(F32))
    in_grad = grad_middle + grad_tokens_norm
    d_qv_bias = lax.psum(grad_bias_own, "cells")
    d_ln_gain, d_ln_shift, d_out_bias, d_up_bias = lax.psum(
        (
            jnp.stack([grad_gain1, grad_gain2]),
            jnp.stack([grad_shift1, grad_shift2]),
            jnp.stack([grad_bias_attn, grad_bias_down]),
            grad_up_bias,
        ),
        ("cells", "seq"),
    )
    return (
        block_out[None], in_grad[None], d_ln_gain, d_ln_shift, d_qkv.astype(F32), d_qv_bias,
        d_out.astype(F32), d_out_bias, d_up, d_up_bias, d_down,
    )


def solution(mesh):
    placed = (
        P("cells", "seq", None), P("cells"), P("cells"), P(), P(), P(None, None, "seq"),
        P(None, "seq"), P("seq", None), P(), P("cells", "seq"), P(), P("cells", "seq"),
        P("cells", "seq", None),
    )
    return jax.shard_map(
        body,
        mesh=mesh,
        in_specs=placed,
        out_specs=(
            P("cells", "seq", None), P("cells", "seq", None), P(), P(), P(None, None, "seq"),
            P(None, "seq"), P("seq", None), P(), P("cells", "seq"), P(), P("cells", "seq"),
        ),
        check_vma=False,
    )
```

time: 1330 us -> 764 us (0.57)
  blocking collectives: 288 us -> 75.5 us
  matrix products: 244 us -> 86.8 us
  local copies, waits for them, and re-layouts: 147 us -> 24.4 us
  waiting for transfers between devices: 570 us -> 458 us
  Pallas kernels: 0 us -> 50 us
  starting transfers between devices: 22 us -> 5.63 us
    all_to_all x3 -> x1, blocking collectives: 211 us -> 15.2 us  [body(): moved = lax.all_to_all(both, 'seq', split_axis=0, concat_axis=0, tiled=True)]
    dot_general x23 -> x12, matrix products: 237 us -> 86.8 us  [the longest x3 22.5 us: dot_nt(): lax.dot_general(a, b, (((1,), (1,)), ((), ())), preferred_element_type=F32)]
    unnamed x16 -> x13, waiting for transfers between devices: 131 us -> 0.72 us
    reduce_scatter x3 -> x6, waiting for transfers between devices: 83.3 us -> 209 us  [the longest x1 71.4 us: body(): lax.psum_scatter(grad_down_unit, 'cells', scatter_dimension=0, tiled=True)]
    psum x1, waiting for transfers between devices: 183 us -> 65.2 us  [body(): lax.psum((grad_qkv_own.astype(BF), grad_out_own.astype(BF)), 'cells')]
    all_gather x6, waiting for transfers between devices: 85 us -> 171 us  [the longest x1 58.1 us: body(): down_unit = lax.all_gather(mine[1], 'cells', axis=0, tiled=True)]
    all_to_all x5 -> x1, waiting for transfers between devices: 87.6 us -> 12.3 us  [body(): lax.all_to_all(unit_parts, 'seq', split_axis=0, concat_axis=0, tiled=True)]
    unnamed x83 -> x38, local copies, waits for them, and re-layouts: 60.8 us -> 8.58 us
  transfers between devices with their start and end apart: 18 -> 14, of which waited for: 12 -> 14; matrix products, arithmetic and copies ran while one was open for 28% -> 13% of each run, Pallas kernels for 0% -> 4%
where the time goes in v1:
time: 764 us; the launch traced here: 754 us
  waiting for transfers between devices  458 us (60%)
  matrix products  86.8 us (11%)
  blocking collectives  75.5 us (10%)
  Pallas kernels  50 us (7%)
  other arithmetic  36.2 us (5%)
  local copies, waits for them, and re-layouts  24.4 us (3%)
  between operations  17.6 us (2%)
    reduce_scatter x1, waiting for transfers between devices, body(): lax.psum_scatter(grad_down_unit, 'cells', scatter_dimension=0, tiled=True)  71.4 us
    psum x1, waiting for transfers between devices, body(): lax.psum((grad_qkv_own.astype(BF), grad_out_own.astype(BF)), 'cells')  65.2 us
    all_gather x1, waiting for transfers between devices, body(): down_unit = lax.all_gather(mine[1], 'cells', axis=0, tiled=True)  58.1 us
    psum x1, blocking collectives, body(): lax.psum((jnp.stack([grad_gain1, grad_gain2]), jnp.stack([grad_shift1, gr...  40.7 us
    reduce_scatter x1, waiting for transfers between devices, body(): lax.psum_scatter(down_terms, 'seq', scatter_dimension=0, tiled=True)  37.2 us
    reduce_scatter x1, waiting for transfers between devices, body(): lax.psum_scatter(normed_terms.astype(BF), 'seq', scatter_dimension=0, til...  33.8 us
    all_gather x1, waiting for transfers between devices, body(): normed_all = lax.all_gather(normed, 'seq', axis=0, tiled=True)  28.8 us
    pallas_call x1, Pallas kernels, attend_back(): pl.pallas_call(attend_back_kernel, name='attend_back', out_shape=jax.Shap...  28.3 us
  transfers between devices with their start and end apart: 14, of which 14 were waited for; matrix products, arithmetic and copies ran while one was open for 13% of the time, Pallas kernels for 4%

profile of v1, /device:TPU:0, one launch (start us, length us, event | category | flops | bytes accessed | tf_op | source)
XLA Modules:
  0.0 754.3 jit_solution(9263721268857702724)
XLA Ops:
  16.3 28.8 %all-gather.8.cloned.1.call-done = bf16[1280,1120]{1,0:T(8,128)(2,1)} async-done(((bf16[320,1120]{1,0:T(8,128)(2,1)}), bf16[1280,1120]{1,0:T(8,128)(2,1)}) %all-gather.8.cloned.1.call-update) | async-done | bytes 2867216 | tf_op jit(solution)/shard_map/all_gather | solution.py:225
  45.1 8.4 %fusion.8.packed_ref = bf16[3,1280,280]{2,1,0:T(8,128)(2,1)} fusion(bf16[3,1120,280]{1,2,0:T(8,128)(2,1)S(1)} %copy-done, bf16[1280,1120]{1,0:T(8,128)(2,1)} %all-gather.8.cloned.1.call-done, f32[3,280]{1,0:T(4,128)S(1)} %maximum_convert_fusion), kind=kOutput, calls=%fused_computation.23 | convolution fusion | flops 2410598400 | bytes 6902560 | tf_op jit(solution)/shard_map/sd,tde->tse/dot_general | solution.py:228
  53.5 21.7 %attend.1 = (bf16[1280,280]{1,0:T(8,128)(2,1)}, f32[5,1,1280]{2,1,0:T(1,128)}) custom-call(s32[1]{0:T(128)S(6)} %copy.79.drop_ref, s32[1]{0:T(128)S(6)} %copy.80.len_ref, bf16[3,1280,280]{2,1,0:T(8,128)(2,1)} %fusion.8.packed_ref), custom_call_target="tpu_custom_call" | custom-call | tf_op jit(solution)/shard_map/attend/pallas_call | solution.py:93
  81.7 15.2 %all_to_all.10 = bf16[4,2,144,280]{3,2,1,0:T(8,128)(2,1)S(1)} all-to-all(bf16[4,2,144,280]{3,2,1,0:T(8,128)(2,1)S(1)} %copy.61), channel_id=1, replica_groups=mesh['cells'=8,'seq'=4] {'seq'}, dimensions={0} | all-to-all | bytes 1290240 | tf_op jit(solution)/shard_map/all_to_all | solution.py:209
  99.1 17.7 %reduce-scatter.7.cloned.1.call-done = bf16[320,1120]{1,0:T(8,128)(2,1)} async-done(((bf16[1280,1120]{1,0:T(8,128)(2,1)}), bf16[320,1120]{1,0:T(8,128)(2,1)}) %reduce-scatter.7.cloned.1.call-update) | async-done | bytes 716816 | tf_op jit(solution)/shard_map/reduce_scatter | solution.py:233
  126.4 27.9 %all-gather.12.cloned.1.call-done = bf16[1152,1120]{1,0:T(8,128)(2,1)} async-done(((bf16[144,1120]{1,0:T(8,128)(2,1)}), bf16[1152,1120]{1,0:T(8,128)(2,1)}) %all-gather.12.cloned.1.call-update) | async-done | bytes 2580496 | tf_op jit(solution)/shard_map/all_gather | solution.py:211
  154.2 28.0 %all-gather.10.cloned.1.call-done = bf16[1280,1120]{1,0:T(8,128)(2,1)} async-done(((bf16[320,1120]{1,0:T(8,128)(2,1)}), bf16[1280,1120]{1,0:T(8,128)(2,1)}) %all-gather.10.cloned.1.call-update) | async-done | bytes 2867216 | tf_op jit(solution)/shard_map/all_gather | solution.py:237
  182.2 9.7 %convolution_add_fusion = f32[1280,1152]{1,0:T(8,128)} fusion(bf16[1280,1120]{1,0:T(8,128)(2,1)} %all-gather.10.cloned.1.call-done, bf16[1152,1120]{1,0:T(8,128)(2,1)} %all-gather.12.cloned.1.call-done, f32[1152]{0:T(1024)S(1)} %add.151), kind=kOutput, calls=%fused_computation | convolution fusion | flops 3304488960 | bytes 11350528 | tf_op jit(solution)/shard_map/dot_general | solution.py:26
  191.9 19.1 %all-gather.18.cloned.1.call-done = bf16[1,1280,1120]{2,1,0:T(8,128)(2,1)} async-done(((bf16[1,320,1120]{2,1,0:T(8,128)(2,1)}), bf16[1,1280,1120]{2,1,0:T(8,128)(2,1)}) %all-gather.18.cloned.1.call-update) | async-done | bytes 2867216 | tf_op jit(solution)/shard_map/all_gather | solution.py:238
  211.0 58.1 %all-gather.14.cloned.1.call-done = bf16[1152,1120]{1,0:T(8,128)(2,1)} async-done(((bf16[144,1120]{1,0:T(8,128)(2,1)}), bf16[1152,1120]{1,0:T(8,128)(2,1)}) %all-gather.14.cloned.1.call-update) | async-done | bytes 2580496 | tf_op jit(solution)/shard_map/all_gather | solution.py:212
  269.1 9.8 %convert_reduce_fusion = (f32[1152]{0:T(1024)S(1)}, bf16[1280,1152]{1,0:T(8,128)(2,1)S(1)}) fusion(f32[1280,1152]{1,0:T(8,128)} %convolution_add_fusion, bf16[1152,1120]{1,0:T(8,128)(2,1)} %all-gather.14.cloned.1.call-done, bf16[1,1280,1120]{2,1,0:T(8,128)(2,1)} %all-gather.18.cloned.1.call-done), kind=kOutput, calls=%fused_computation.18 | convolution fusion | flops 3335453696 | bytes 14299648 | tf_op jit(solution)/shard_map/dot_general | solution.py:26
  286.6 10.4 %convolution_convert_fusion.3 = bf16[1280,1120]{1,0:T(8,128)(2,1)} fusion(bf16[1152,1120]{1,0:T(8,128)(2,1)} %all-gather.14.cloned.1.call-done, f32[1280,1152]{1,0:T(8,128)} %convolution_add_fusion), kind=kOutput, calls=%fused_computation.8 | convolution fusion | flops 3317719040 | bytes 11345920 | tf_op jit(solution)/shard_map/dot_general | solution.py:22
  297.0 24.5 %reduce-scatter.11.cloned.1.call-done = bf16[320,1120]{1,0:T(8,128)(2,1)} async-done(((bf16[1280,1120]{1,0:T(8,128)(2,1)}), bf16[320,1120]{1,0:T(8,128)(2,1)}) %reduce-scatter.11.cloned.1.call-update) | async-done | bytes 716816 | tf_op jit(solution)/shard_map/reduce_scatter | solution.py:246
  323.5 37.2 %reduce-scatter.9.cloned.1.call-done = bf16[320,1120]{1,0:T(8,128)(2,1)} async-done(((bf16[1280,1120]{1,0:T(8,128)(2,1)}), bf16[320,1120]{1,0:T(8,128)(2,1)}) %reduce-scatter.9.cloned.1.call-update) | async-done | bytes 716816 | tf_op jit(solution)/shard_map/reduce_scatter | solution.py:247
  374.7 9.8 %convolution_convert_fusion = bf16[1152,1120]{1,0:T(8,128)(2,1)} fusion(bf16[1,1280,1120]{2,1,0:T(8,128)(2,1)} %all-gather.18.cloned.1.call-done, f32[1280,1152]{1,0:T(8,128)} %convolution_add_fusion), kind=kOutput, calls=%fused_computation.5 | convolution fusion | flops 3317575680 | bytes 11345920 | tf_op jit(solution)/shard_map/dot_general | solution.py:30
  384.6 8.9 %all-gather.16.cloned.1.call-done = bf16[1280,1120]{1,0:T(8,128)(2,1)} async-done(((bf16[320,1120]{1,0:T(8,128)(2,1)}), bf16[1280,1120]{1,0:T(8,128)(2,1)}) %all-gather.16.cloned.1.call-update) | async-done | bytes 2867216 | tf_op jit(solution)/shard_map/all_gather | solution.py:260
  397.9 28.3 %attend_back.1 = bf16[3,1280,280]{2,1,0:T(8,128)(2,1)} custom-call(s32[1]{0:T(128)S(6)} %copy.79.drop_ref, s32[1]{0:T(128)S(6)} %copy.80.len_ref, bf16[3,1280,280]{2,1,0:T(8,128)(2,1)} %fusion.8.packed_ref, bf16[1280,280]{1,0:T(8,128)(2,1)} %get-tuple-element.13.out_ref, f32[5,1,1280]{2,1,0:T(1,128)} %get-tuple-element.14.lse_ref, ...), custom_call_target="tpu_custom_call" | custom-call | tf_op jit(solution)/shard_map/attend_back/pallas_call | solution.py:178
  443.5 24.8 %reduce-scatter.15.cloned.1.call-done = bf16[144,1120]{1,0:T(8,128)(2,1)} async-done(((bf16[1152,1120]{1,0:T(8,128)(2,1)}), bf16[144,1120]{1,0:T(8,128)(2,1)}) %reduce-scatter.15.cloned.1.call-update) | async-done | bytes 322576 | tf_op jit(solution)/shard_map/reduce_scatter | solution.py:264
  470.5 71.4 %reduce-scatter.17.cloned.1.call-done = bf16[144,1120]{1,0:T(8,128)(2,1)} async-done(((bf16[1152,1120]{1,0:T(8,128)(2,1)}), bf16[144,1120]{1,0:T(8,128)(2,1)}) %reduce-scatter.17.cloned.1.call-update) | async-done | bytes 322576 | tf_op jit(solution)/shard_map/reduce_scatter | solution.py:265
  551.9 12.3 %all-to-all-done.1 = bf16[4,2,144,280]{3,2,1,0:T(8,128)(2,1)} async-done(((bf16[4,2,144,280]{3,2,1,0:T(8,128)(2,1)}), bf16[4,2,144,280]{3,2,1,0:T(8,128)(2,1)}, u32[]{:S(2)}, u32[]{:S(2)}) %all-to-all-start.1) | async-done | bytes 645152 | tf_op jit(solution)/shard_map/all_to_all | solution.py:277
  575.7 19.5 %psum.52 = f32[2,280]{1,0:T(2,128)} all-reduce(f32[2,280]{1,0:T(2,128)S(1)} %convert_reduce_fusion.1), channel_id=1, replica_groups=mesh['cells'=8,'seq'=4] {'cells'}, use_global_device_ids=true, to_apply=%region_20.21 | all-reduce | flops 560 | bytes 4480 | tf_op jit(solution)/shard_map/psum | solution.py:284
  595.2 65.2 %all-reduce.7.cloned.1.call-done = (bf16[3,1120,280]{1,2,0:T(8,128)(2,1)}, bf16[280,1120]{1,0:T(8,128)(2,1)}) async-done(((bf16[3,1120,280]{1,2,0:T(8,128)(2,1)}, bf16[280,1120]{1,0:T(8,128)(2,1)}), (bf16[3,1120,280]{1,2,0:T(8,128)(2,1)}, bf16[280,1120]{1,0:T(8,128)(2,1)})) %all-reduce.7.cloned.1.call-update) | async-done | bytes 2508816 | tf_op jit(solution)/shard_map/psum | solution.py:281
  665.0 33.8 %reduce-scatter.13.cloned.1.call-done = bf16[320,1120]{1,0:T(8,128)(2,1)} async-done(((bf16[1280,1120]{1,0:T(8,128)(2,1)}), bf16[320,1120]{1,0:T(8,128)(2,1)}) %reduce-scatter.13.cloned.1.call-update) | async-done | bytes 716816 | tf_op jit(solution)/shard_map/reduce_scatter | solution.py:272
  702.4 40.7 %all-reduce.3 = (f32[2,1120]{1,0:T(2,128)}, f32[2,1120]{1,0:T(2,128)}, f32[2,1120]{1,0:T(2,128)}, f32[4480]{0:T(1024)}) all-reduce(f32[2,1120]{1,0:T(2,128)S(1)} %pad_maximum_fusion.1, f32[2,1120]{1,0:T(2,128)S(1)} %pad_maximum_fusion.2, f32[2,1120]{1,0:T(2,128)S(1)} %pad_maximum_fusion.3, ...), channel_id=1, replica_groups=mesh['cells'=8,'seq'=4] {'cells','seq'}, use_global_device_ids=true, to_apply=%region_14.15 | all-reduce | flops 11200 | bytes 89600 | tf_op jit(solution)/shard_map/psum | solution.py:285
  (141 shorter events, 105.7 us)
Async XLA Ops:
  8.0 37.1 %copy-start = (bf16[3,1120,280]{1,2,0:T(8,128)(2,1)S(1)}, bf16[3,1120,280]{1,2,0:T(8,128)(2,1)}, u32[]{:S(2)}) copy-start(bf16[3,1120,280]{1,2,0:T(8,128)(2,1)} %param.18) | copy-start | bytes 5644804
  8.0 8.2 %copy-start.12 = (bf16[2,280]{1,0:T(2,128)(2,1)S(1)}, bf16[2,280]{1,0:T(2,128)(2,1)}, u32[]{:S(2)}) copy-start(bf16[2,280]{1,0:T(2,128)(2,1)} %param.19) | copy-start | bytes 3364
  8.0 37.1 %all-gather.8.cloned.1.call-start = ((), (), s32[]{:S(2)}) async-start(), calls=%async_computation.8 | async-start | bytes 3686400 | tf_op jit(solution)/shard_map/all_gather | solution.py:225
  14.8 102.0 %reduce-scatter.7.cloned.1.call-start = ((), (), s32[]{:S(2)}) async-start(), calls=%async_computation.9 | async-start | bytes 3686400 | tf_op jit(solution)/shard_map/reduce_scatter | solution.py:233
  53.5 21.7 %copy-start.15 = (bf16[280,1120]{1,0:T(8,128)(2,1)S(1)}, bf16[280,1120]{1,0:T(8,128)(2,1)}, u32[]{:S(2)}) copy-start(bf16[280,1120]{1,0:T(8,128)(2,1)} %param.20) | copy-start | bytes 1881604
  79.8 74.4 %all-gather.12.cloned.1.call-start = ((), (), s32[]{:S(2)}) async-start(), calls=%async_computation.11 | async-start | bytes 2985984 | tf_op jit(solution)/shard_map/all_gather | solution.py:211
  81.7 17.4 %copy-start.13 = (bf16[2,1120]{1,0:T(2,128)(2,1)S(1)}, bf16[2,1120]{1,0:T(2,128)(2,1)}, u32[]{:S(2)}) copy-start(bf16[2,1120]{1,0:T(2,128)(2,1)} %param.21) | copy-start | bytes 13444
  81.7 35.1 %copy-start.1 = (bf16[1,320,1120]{2,1,0:T(8,128)(2,1)S(1)}, bf16[1,320,1120]{2,1,0:T(8,128)(2,1)}, u32[]{:S(2)}) copy-start(bf16[1,320,1120]{2,1,0:T(8,128)(2,1)} %param.13) | copy-start | bytes 2150404
  99.0 83.2 %all-gather.10.cloned.1.call-start = ((), (), s32[]{:S(2)}) async-start(), calls=%async_computation.10 | async-start | bytes 3686400 | tf_op jit(solution)/shard_map/all_gather | solution.py:237
  119.9 6.1 copy-start.11
  121.3 89.7 %all-gather.18.cloned.1.call-start = ((), (), s32[]{:S(2)}) async-start(), calls=%async_computation.19 | async-start | bytes 3686400 | tf_op jit(solution)/shard_map/all_gather | solution.py:238
  121.8 147.2 %all-gather.14.cloned.1.call-start = ((), (), s32[]{:S(2)}) async-start(), calls=%async_computation.12 | async-start | bytes 2985984 | tf_op jit(solution)/shard_map/all_gather | solution.py:212
  126.0 195.6 %reduce-scatter.11.cloned.1.call-start = ((), (), s32[]{:S(2)}) async-start(), calls=%async_computation.14 | async-start | bytes 3686400 | tf_op jit(solution)/shard_map/reduce_scatter | solution.py:246
  269.1 11.4 %copy-start.14 = (bf16[1152,1120]{1,0:T(8,128)(2,1)S(1)}, bf16[1152,1120]{1,0:T(8,128)(2,1)}, u32[]{:S(2)}) copy-start(bf16[1152,1120]{1,0:T(8,128)(2,1)} %all-gather.12.cloned.1.call-done) | copy-start | bytes 7741444
  286.1 74.6 %reduce-scatter.9.cloned.1.call-start = ((), (), s32[]{:S(2)}) async-start(), calls=%async_computation.13 | async-start | bytes 3686400 | tf_op jit(solution)/shard_map/reduce_scatter | solution.py:247
  297.0 96.5 %all-gather.16.cloned.1.call-start = ((), (), s32[]{:S(2)}) async-start(), calls=%async_computation.15 | async-start | bytes 3686400 | tf_op jit(solution)/shard_map/all_gather | solution.py:260
  360.7 4.2 copy-start.4
  366.1 102.1 %reduce-scatter.15.cloned.1.call-start = ((), (), s32[]{:S(2)}) async-start(), calls=%async_computation.17 | async-start | bytes 2985984 | tf_op jit(solution)/shard_map/reduce_scatter | solution.py:264
  374.5 167.4 %reduce-scatter.17.cloned.1.call-start = ((), (), s32[]{:S(2)}) async-start(), calls=%async_computation.18 | async-start | bytes 2985984 | tf_op jit(solution)/shard_map/reduce_scatter | solution.py:265
  384.5 276.0 %all-reduce.7.cloned.1.call-start = ((), (), s32[]{:S(2)}) async-start(), calls=%async_computation.20 | async-start | bytes 5160960 | tf_op jit(solution)/shard_map/psum | solution.py:281
  397.9 28.3 %copy-start.8 = (bf16[1280,280]{1,0:T(8,128)(2,1)S(1)}, bf16[1280,280]{1,0:T(8,128)(2,1)}, u32[]{:S(2)}) copy-start(bf16[1280,280]{1,0:T(8,128)(2,1)} %get-tuple-element.13.out_ref) | copy-start | bytes 2150404
  436.4 262.3 %reduce-scatter.13.cloned.1.call-start = ((), (), s32[]{:S(2)}) async-start(), calls=%async_computation.16 | async-start | bytes 3686400 | tf_op jit(solution)/shard_map/reduce_scatter | solution.py:272
  470.5 80.9 %copy-start.5 = (bf16[1,320,1120]{2,1,0:T(8,128)(2,1)S(1)}, bf16[1,320,1120]{2,1,0:T(8,128)(2,1)}, u32[]{:S(2)}) copy-start(bf16[1,320,1120]{2,1,0:T(8,128)(2,1)} %param.25) | copy-start | bytes 2150404
  547.2 17.0 %all-to-all-start.1 = ((bf16[4,2,144,280]{3,2,1,0:T(8,128)(2,1)}), bf16[4,2,144,280]{3,2,1,0:T(8,128)(2,1)}, u32[]{:S(2)}, u32[]{:S(2)}) async-start(bf16[4,2,144,280]{3,2,1,0:T(8,128)(2,1)} %maximum_bitcast_fusion), calls=%async_computation.7 | async-start | bytes 1769472 | tf_op jit(solution)/shard_map/all_to_all | solution.py:277
  (7 other events, 14.5 us)
Sparse Core Ops, SparseCore 0:
  14.9 30.1 all-gather.7
  79.9 36.8 reduce-scatter.6
  286.2 35.2 reduce-scatter.10
  324.0 36.7 reduce-scatter.8
Sparse Core Ops, SparseCore 1:
  99.1 55.1 all-gather.11
  156.3 25.8 all-gather.9
  183.7 27.2 all-gather.17
  214.0 55.0 all-gather.13
  366.2 27.2 all-gather.15
  397.6 70.6 reduce-scatter.14
  471.8 70.0 reduce-scatter.16
  546.5 113.9 all-reduce.6
  663.0 35.6 reduce-scatter.12

commit v2 on v1

v2 whole, which is shorter than its diff:
```python
import functools
import math

import jax
import jax.numpy as jnp
from jax import lax
from jax.experimental import pallas as pl
from jax.experimental.pallas import tpu as pltpu
from jax.sharding import PartitionSpec as P

HEADS = 20
HD = 56
LANES = 128
epsilon = 1e-05
masked = -1e30
BF = jnp.bfloat16
F32 = jnp.float32
VMEM_LIMIT = 63 * 1024 * 1024
MESH = pl.DeviceIdType.MESH
VM = pl.BlockSpec(memory_space=pltpu.VMEM)
SM = pl.BlockSpec(memory_space=pltpu.SMEM)
CHUNKS = 2


def dot_nn(a, b):
    return lax.dot_general(a, b, (((1,), (0,)), ((), ())), preferred_element_type=F32)


def dot_nt(a, b):
    return lax.dot_general(a, b, (((1,), (1,)), ((), ())), preferred_element_type=F32)


def dot_tn(a, b):
    return lax.dot_general(a, b, (((0,), (0,)), ((), ())), preferred_element_type=F32)


def normalize(rows):
    centre = jnp.mean(rows, axis=-1, keepdims=True)
    offsets = rows - centre
    spread = jnp.mean(offsets * offsets, axis=-1, keepdims=True)
    inverse = lax.rsqrt(spread + epsilon)
    return offsets * inverse, inverse


def normalize_back(grad, unit, inverse, gain):
    scaled = grad * gain
    first = jnp.mean(scaled, axis=-1, keepdims=True)
    second = jnp.mean(scaled * unit, axis=-1, keepdims=True)
    return (scaled - first - unit * second) * inverse


def column_sum(values):
    return jnp.sum(values, axis=0, keepdims=True)


class Group:
    def __init__(self, send_sem, recv_sem):
        here = lax.axis_index("seq")
        self.here = here
        self.send_sem, self.recv_sem = send_sem, recv_sem
        self.mate, self.peer, self.far = self.other(1), self.other(2), self.other(3)
        self.used = 0

    def other(self, step):
        high = lax.rem(self.here // 2 + step // 2, 2)
        low = lax.rem(lax.rem(self.here, 2) + lax.rem(step, 2), 2)
        return high * 2 + low

    def barrier(self, members):
        sem = pltpu.get_barrier_semaphore()
        for member in members:
            pl.semaphore_signal(sem, inc=1, device_id={"seq": member}, device_id_type=MESH)
        pl.semaphore_wait(sem, len(members))

    def take(self, count):
        first = self.used
        self.used += count
        return first

    def copy(self, src, dst, index, member):
        return pltpu.make_async_remote_copy(
            src_ref=src,
            dst_ref=dst,
            send_sem=self.send_sem.at[index],
            recv_sem=self.recv_sem.at[index],
            device_id={"seq": member},
            device_id_type=MESH,
        )


class Gather:
    def __init__(self, group, buf):
        self.group, self.buf = group, buf
        self.rows = buf.shape[0] // 4
        self.chunk = self.rows // CHUNKS
        self.first = group.take(3 * CHUNKS)

    def at(self, member, k):
        start = pl.multiple_of(member * self.rows + k * self.chunk, 16)
        return self.buf.at[pl.ds(start, self.chunk), :]

    def descriptor(self, role, k, member_rows):
        ref = self.at(member_rows, k)
        to = self.group.peer if role == 1 else self.group.mate
        return self.group.copy(ref, ref, self.first + role * CHUNKS + k, to)

    def start(self, k):
        self.descriptor(1, k, self.group.here).start()
        self.descriptor(0, k, self.group.here).start()

    def forward(self):
        for k in range(CHUNKS):
            self.descriptor(1, k, self.group.peer).wait_recv()
            self.descriptor(2, k, self.group.peer).start()

    def wait_mate(self):
        for k in range(CHUNKS):
            self.descriptor(0, k, self.group.mate).wait_recv()

    def wait_far(self):
        for k in range(CHUNKS):
            self.descriptor(2, k, self.group.far).wait_recv()

    def finish(self):
        for k in range(CHUNKS):
            self.descriptor(1, k, self.group.here).wait_send()
            self.descriptor(0, k, self.group.here).wait_send()
            self.descriptor(2, k, self.group.peer).wait_send()


class Scatter:
    def __init__(self, group, out, land):
        self.group, self.out, self.land = group, out, land
        self.chunk = out.shape[1] // CHUNKS
        self.first = group.take(3 * CHUNKS)

    def descriptor(self, role, k):
        part = pl.ds(k * self.chunk, self.chunk)
        to = self.group.peer if role == 1 else self.group.mate
        return self.group.copy(
            self.out.at[role, part], self.land.at[role, part], self.first + role * CHUNKS + k, to
        )

    def send(self, role, k, values):
        self.out[role, pl.ds(k * self.chunk, self.chunk), :] = values.astype(BF)
        self.descriptor(role, k).start()

    def arrived(self, role, k):
        self.descriptor(role, k).wait_recv()
        return self.land[role, pl.ds(k * self.chunk, self.chunk), :].astype(F32)

    def finish(self):
        for role in range(3):
            for k in range(CHUNKS):
                self.descriptor(role, k).wait_send()


def seq_call(kernel, collective, copies, scratch, out_shape, in_specs, **kwargs):
    return pl.pallas_call(
        kernel,
        out_shape=out_shape,
        in_specs=in_specs,
        out_specs=jax.tree.map(lambda _: VM, out_shape),
        scratch_shapes=list(scratch)
        + [pltpu.SemaphoreType.DMA((copies,)), pltpu.SemaphoreType.DMA((copies,))],
        compiler_params=pltpu.CompilerParams(
            collective_id=collective, has_side_effects=True, vmem_limit_bytes=VMEM_LIMIT
        ),
        **kwargs,
    )


def project_kernel(
    tok_ref, gain_ref, shift_ref, w_ref, bias_ref, up_ref, down_ref,
    normed_ref, packed_ref, wcat_ref, units_ref,
    wsend, wland, send_sem, recv_sem,
):
    group = Group(send_sem, recv_sem)
    rows = tok_ref.shape[0]
    share, part = wsend.shape[1], up_ref.shape[1]
    unit_rows = up_ref.shape[0]
    gather = Gather(group, normed_ref)
    first = group.take(3)
    chunk = rows // CHUNKS
    for k in range(CHUNKS):
        values = tok_ref[pl.ds(k * chunk, chunk), :].astype(F32)
        unit, _ = normalize(values)
        start = pl.multiple_of(group.here * rows + k * chunk, 16)
        normed_ref[pl.ds(start, chunk), :] = (unit * gain_ref[...] + shift_ref[...]).astype(BF)
    wsend[...] = jnp.zeros_like(wsend)
    for t in range(4):
        count = max(min(share, unit_rows - t * share), 0)
        if count:
            wsend[t, :count, :part] = up_ref[t * share : t * share + count, :]
            wsend[t, :count, part : 2 * part] = down_ref[t * share : t * share + count, :]
    group.barrier([group.mate, group.peer, group.far])
    for k in range(CHUNKS):
        gather.start(k)

    def exchange(step):
        to = group.other(step)
        return group.copy(wsend.at[to], wland.at[group.here], first + step - 1, to)

    for step in (2, 3, 1):
        exchange(step).start()
    for t in range(3):
        wcat_ref[:, t * part : (t + 1) * part] = w_ref[t]

    def project(member):
        start = pl.multiple_of(member * rows, 16)
        x = normed_ref[pl.ds(start, rows), :]
        packed_ref[pl.ds(start, rows), :] = (dot_nn(x, wcat_ref[...]) + bias_ref[...]).astype(BF)

    project(group.here)
    gather.wait_mate()
    project(group.mate)
    gather.forward()
    project(group.peer)
    gather.wait_far()
    project(group.far)
    wland[group.here] = wsend[group.here]
    for step in (1, 2, 3):
        source = group.other(step)
        group.copy(wsend.at[source], wland.at[source], first + step - 1, source).wait_recv()
    for which in range(2):
        for t in range(4):
            units_ref[which, :, t * part : (t + 1) * part] = wland[t][
                :, which * part : (which + 1) * part
            ]
    for step in (1, 2, 3):
        exchange(step).wait_send()
    gather.finish()


def project(tokens, gain, shift, w_qkv, bias, w_up, w_down, share):
    rows, width = tokens.shape
    part = w_up.shape[1]
    wide = -(-2 * part // LANES) * LANES
    return seq_call(
        project_kernel, 1, 3 * CHUNKS + 3,
        [pltpu.VMEM((4, share, wide), BF)] * 2,
        (
            jax.ShapeDtypeStruct((4 * rows, width), BF),
            jax.ShapeDtypeStruct((4 * rows, 3 * part), BF),
            jax.ShapeDtypeStruct((width, 3 * part), BF),
            jax.ShapeDtypeStruct((2, share, width), BF),
        ),
        [VM] * 7,
        name="project",
    )(tokens, gain, shift, w_qkv, bias, w_up, w_down)


def block_size(length):
    return 256 if length % 256 == 0 else length


def attend_kernel(
    drop_ref, len_ref, packed_ref, cot_ref, out_ref, lse_ref, cots_ref,
    q_sc, k_sc, v_sc, o_sc, send_sem, recv_sem,
):
    heads, length, _ = q_sc.shape
    block = block_size(length)
    factor = (1.0 / math.sqrt(HD)) * math.log2(math.e)
    dropped, limit = drop_ref[0], len_ref[0]
    group = Group(send_sem, recv_sem)
    gather = Gather(group, cots_ref)
    rows = cot_ref.shape[0]
    cots_ref[pl.ds(pl.multiple_of(group.here * rows, 16), rows), :] = cot_ref[...]
    for t, sc in enumerate((q_sc, k_sc, v_sc)):
        sc[...] = jnp.zeros_like(sc)
        for h in range(heads):
            sc[h, :, :HD] = packed_ref[:, (t * heads + h) * HD : (t * heads + h + 1) * HD]
    group.barrier([group.mate, group.peer])
    for k in range(CHUNKS):
        gather.start(k)
    key = lax.broadcasted_iota(jnp.int32, (1, length), 1)
    bias = jnp.where((key >= dropped) & (key < limit), 0.0, masked)

    def head(h, carry):
        for i in range(length // block):
            width = (i + 1) * block
            q = q_sc[h, pl.ds(i * block, block), :]
            raw = dot_nt(q, k_sc[h, pl.ds(0, width), :])
            row = i * block + lax.broadcasted_iota(jnp.int32, (block, block), 0)
            col = i * block + lax.broadcasted_iota(jnp.int32, (block, block), 1)
            ok = (col <= row) & (col < limit)
            if i == 0:
                ok = ok & ((col >= dropped) | (col == row))
            last = jnp.where(ok, raw[:, i * block :], masked)
            if i:
                raw = jnp.concatenate([raw[:, : i * block] + bias[:, : i * block], last], axis=1)
            else:
                raw = last
            top = jnp.max(raw, axis=1, keepdims=True) * factor
            weights = jnp.exp2(raw * factor - top)
            total = jnp.sum(weights, axis=1, keepdims=True)
            probs = (weights * (1.0 / total)).astype(BF)
            out = dot_nn(probs, v_sc[h, pl.ds(0, width), :])
            o_sc[h, pl.ds(i * block, block), :] = out.astype(BF)
            stat = jnp.broadcast_to(top + jnp.log2(total), (block, LANES))
            lse_ref[h, 0:1, pl.ds(i * block, block)] = jnp.transpose(stat)[0:1, :]
        return carry

    lax.fori_loop(0, heads - 1, head, 0)
    gather.forward()
    head(heads - 1, 0)
    for h in range(heads):
        out_ref[:, h * HD : (h + 1) * HD] = o_sc[h, :, :HD]
    gather.wait_mate()
    gather.wait_far()
    gather.finish()


def attend(packed, cot, drop_counts, lengths):
    length, width = packed.shape
    heads = width // (3 * HD)
    return seq_call(
        attend_kernel, 2, 3 * CHUNKS,
        [pltpu.VMEM((heads, length, LANES), BF)] * 4,
        (
            jax.ShapeDtypeStruct((length, heads * HD), BF),
            jax.ShapeDtypeStruct((heads, 1, length), F32),
            jax.ShapeDtypeStruct((length, cot.shape[1]), BF),
        ),
        [SM, SM, VM, VM],
        name="attend",
    )(drop_counts, lengths, packed, cot)


GELU_A = math.sqrt(2.0 / math.pi)
GELU_B = 0.044715


def middle_kernel(
    att_ref, tok_ref, cots_ref, wout_ref, up_ref, down_ref, upb_ref, bias_ref, gain_ref, shift_ref,
    mid_ref, terms_ref, gmid_ref, gbranch_ref, gup_ref, gdown_ref, gsum_ref, gupb_ref,
    all_sc, act_sc, ghid_sc, part_sc, out_sc, land_sc, out2_sc, land2_sc, send_sem, recv_sem,
):
    group = Group(send_sem, recv_sem)
    rows, width = tok_ref.shape
    units = up_ref.shape[0]
    chunk = rows // CHUNKS
    scatter = Scatter(group, out_sc, land_sc)
    gather = Gather(group, all_sc)
    scatter2 = Scatter(group, out2_sc, land2_sc)
    group.barrier([group.mate, group.peer])

    def terms(member, k):
        start = pl.multiple_of(member * rows + k * chunk, 16)
        return dot_nn(att_ref[pl.ds(start, chunk), :], wout_ref[...])

    for k in range(CHUNKS):
        scatter.send(0, k, terms(group.far, k))
    for k in range(CHUNKS):
        scatter.send(1, k, terms(group.peer, k) + scatter.arrived(0, k))
    for k in range(CHUNKS):
        scatter.send(2, k, terms(group.mate, k))
    for k in range(CHUNKS):
        part = pl.ds(k * chunk, chunk)
        total = terms(group.here, k) + scatter.arrived(2, k) + scatter.arrived(1, k)
        middle = tok_ref[part, :].astype(F32) + (total + bias_ref[0:1, :])
        mid_ref[part, :] = middle
        unit, _ = normalize(middle)
        start = pl.multiple_of(group.here * rows + k * chunk, 16)
        all_sc[pl.ds(start, chunk), :] = (unit * gain_ref[...] + shift_ref[...]).astype(BF)
        gather.start(k)

    gupb_ref[...] = jnp.zeros_like(gupb_ref)

    def feed(t, carry):
        @pl.when(t == 1)
        def _():
            gather.wait_mate()

        @pl.when(t == 2)
        def _():
            gather.forward()

        @pl.when(t == 3)
        def _():
            gather.wait_far()

        here = pl.ds(pl.multiple_of(group.other(t) * rows, 16), rows)
        hidden = dot_nt(all_sc[here, :], up_ref[...]) + upb_ref[...]
        square = hidden * hidden
        tanh = jnp.tanh(GELU_A * hidden * (1.0 + GELU_B * square))
        half = 0.5 * (1.0 + tanh)
        act_sc[here, :] = (hidden * half).astype(BF)
        slope = half + 0.5 * hidden * (1.0 - tanh * tanh) * (
            GELU_A * (1.0 + (3.0 * GELU_B) * square)
        )
        ghid = (dot_nt(cots_ref[here, :], down_ref[...]) * slope).astype(BF)
        ghid_sc[here, :] = ghid
        gupb_ref[...] += column_sum(ghid.astype(F32))
        part_sc[t] = dot_nn(ghid, up_ref[...])
        terms_ref[here, :] = dot_nn(act_sc[here, :], down_ref[...]).astype(BF)
        return carry

    lax.fori_loop(0, 4, feed, 0)
    for k in range(CHUNKS):
        scatter2.send(0, k, part_sc[3, pl.ds(k * chunk, chunk), :])
    for k in range(CHUNKS):
        scatter2.send(2, k, part_sc[1, pl.ds(k * chunk, chunk), :])
    for k in range(CHUNKS):
        scatter2.send(1, k, part_sc[2, pl.ds(k * chunk, chunk), :] + scatter2.arrived(0, k))

    step = units // 3 if units % (3 * LANES) == 0 else units

    def weights(u, carry):
        mine = pl.ds(pl.multiple_of(u * step, LANES), step)
        gdown_ref[mine, :] = dot_tn(act_sc[:, mine], cots_ref[...]).astype(BF)
        gup_ref[mine, :] = dot_tn(ghid_sc[:, mine], all_sc[...]).astype(BF)
        return carry

    lax.fori_loop(0, units // step, weights, 0)
    sums = [jnp.zeros((1, width), F32)] * 4
    for k in range(CHUNKS):
        part = pl.ds(k * chunk, chunk)
        grad = part_sc[0, part, :] + scatter2.arrived(2, k) + scatter2.arrived(1, k)
        unit, inverse = normalize(mid_ref[part, :])
        start = pl.multiple_of(group.here * rows + k * chunk, 16)
        cot = cots_ref[pl.ds(start, chunk), :].astype(F32)
        gmid = cot + normalize_back(grad, unit, inverse, gain_ref[...])
        gmid_ref[part, :] = gmid
        gbranch = gmid.astype(BF)
        gbranch_ref[part, :] = gbranch
        news = (grad * unit, grad, gbranch.astype(F32), cot)
        sums = [a + column_sum(b) for a, b in zip(sums, news)]
    for i, value in enumerate(sums):
        gsum_ref[i : i + 1, :] = value
    scatter.finish()
    scatter2.finish()
    gather.finish()


def middle_call(attended, tokens, cots, w_out, up, down, up_bias, biases, gain, shift):
    rows, width = tokens.shape
    units = up.shape[0]
    return seq_call(
        middle_kernel, 3, 9 * CHUNKS,
        [
            pltpu.VMEM((4 * rows, width), BF),
            pltpu.VMEM((4 * rows, units), BF),
            pltpu.VMEM((4 * rows, units), BF),
            pltpu.VMEM((4, rows, width), F32),
        ]
        + [pltpu.VMEM((3, rows, width), BF)] * 4,
        (
            jax.ShapeDtypeStruct((rows, width), F32),
            jax.ShapeDtypeStruct((4 * rows, width), BF),
            jax.ShapeDtypeStruct((rows, width), F32),
            jax.ShapeDtypeStruct((rows, width), BF),
            jax.ShapeDtypeStruct((units, width), BF),
            jax.ShapeDtypeStruct((units, width), BF),
            jax.ShapeDtypeStruct((4, width), F32),
            jax.ShapeDtypeStruct((1, units), F32),
        ),
        [VM] * 10,
        name="middle",
    )(attended, tokens, cots, w_out, up, down, up_bias, biases, gain, shift)


def branch_back_kernel(
    gbranch_ref, att_ref, wout_ref, gatt_ref, gout_ref, all_sc, send_sem, recv_sem
):
    group = Group(send_sem, recv_sem)
    rows = gbranch_ref.shape[0]
    gather = Gather(group, all_sc)
    all_sc[pl.ds(pl.multiple_of(group.here * rows, 16), rows), :] = gbranch_ref[...]
    group.barrier([group.mate, group.peer])
    for k in range(CHUNKS):
        gather.start(k)

    def back(member):
        here = pl.ds(pl.multiple_of(member * rows, 16), rows)
        gatt_ref[here, :] = dot_nt(all_sc[here, :], wout_ref[...]).astype(BF)

    back(group.here)
    gather.wait_mate()
    back(group.mate)
    gather.forward()
    back(group.peer)
    gather.wait_far()
    back(group.far)
    gout_ref[...] = dot_tn(att_ref[...], all_sc[...]).astype(BF)
    gather.finish()


def branch_back(gbranch, attended, w_out):
    rows, width = gbranch.shape
    return seq_call(
        branch_back_kernel, 4, 3 * CHUNKS,
        [pltpu.VMEM((4 * rows, width), BF)],
        (
            jax.ShapeDtypeStruct(attended.shape, BF),
            jax.ShapeDtypeStruct(w_out.shape, BF),
        ),
        [VM] * 3,
        name="branch_back",
    )(gbranch, attended, w_out)


def attend_back_kernel(
    drop_ref, len_ref, packed_ref, out_ref, lse_ref, gout_ref, gpacked_ref,
    q_sc, k_sc, v_sc, g_sc, delta_sc, dq_sc, dk_sc, dv_sc,
):
    heads, length, _ = q_sc.shape
    block = block_size(length)
    scale = 1.0 / math.sqrt(HD)
    factor = scale * math.log2(math.e)
    dropped, limit = drop_ref[0], len_ref[0]
    for t, sc in enumerate((q_sc, k_sc, v_sc)):
        sc[...] = jnp.zeros_like(sc)
        for h in range(heads):
            sc[h, :, :HD] = packed_ref[:, (t * heads + h) * HD : (t * heads + h + 1) * HD]
    g_sc[...] = jnp.zeros_like(g_sc)
    for h in range(heads):
        part = slice(h * HD, (h + 1) * HD)
        g = gout_ref[:, part]
        g_sc[h, :, :HD] = g
        prod = jnp.sum(g.astype(F32) * out_ref[:, part].astype(F32), axis=1, keepdims=True)
        delta_sc[h, 0:1, :] = jnp.transpose(jnp.broadcast_to(prod, (length, LANES)))[0:1, :]
    key = lax.broadcasted_iota(jnp.int32, (length, 1), 0)
    bias = jnp.where((key >= dropped) & (key < limit), 0.0, masked)

    def head(h, carry):
        dq_sc[h] = jnp.zeros((length, LANES), F32)
        for j in range(length // block):
            low = j * block
            rest = length - low
            k = k_sc[h, pl.ds(low, block), :]
            v = v_sc[h, pl.ds(low, block), :]
            q = q_sc[h, pl.ds(low, rest), :]
            g = g_sc[h, pl.ds(low, rest), :]
            raw = dot_nt(k, q) * factor
            row = low + lax.broadcasted_iota(jnp.int32, (block, block), 1)
            col = low + lax.broadcasted_iota(jnp.int32, (block, block), 0)
            ok = (col <= row) & (col < limit)
            if j == 0:
                ok = ok & ((col >= dropped) | (col == row))
            first = jnp.where(ok, raw[:, :block], masked)
            if rest > block:
                raw = jnp.concatenate([first, raw[:, block:] + bias[low : low + block]], axis=1)
            else:
                raw = first
            probs = jnp.exp2(raw - lse_ref[h, 0:1, pl.ds(low, rest)])
            gprobs = dot_nt(v, g)
            gscores = (probs * (gprobs - delta_sc[h, 0:1, pl.ds(low, rest)])).astype(BF)
            dv_sc[h, pl.ds(low, block), :] = dot_nn(probs.astype(BF), g).astype(BF)
            dk_sc[h, pl.ds(low, block), :] = (dot_nn(gscores, q) * scale).astype(BF)
            dq_sc[h, pl.ds(low, rest), :] += dot_tn(gscores, k)
        return carry

    lax.fori_loop(0, heads, head, 0)
    for h in range(heads):
        for t, values in enumerate(
            ((dq_sc[h, :, :HD] * scale).astype(BF), dk_sc[h, :, :HD], dv_sc[h, :, :HD])
        ):
            gpacked_ref[:, (t * heads + h) * HD : (t * heads + h + 1) * HD] = values


def attend_back(packed, attended, lse, grad_out, drop_counts, lengths):
    length, width = packed.shape
    heads = width // (3 * HD)
    return pl.pallas_call(
        attend_back_kernel,
        name="attend_back",
        out_shape=jax.ShapeDtypeStruct((length, width), BF),
        in_specs=[SM, SM, VM, VM, VM, VM],
        out_specs=VM,
        scratch_shapes=[pltpu.VMEM((heads, length, LANES), BF)] * 4
        + [pltpu.VMEM((heads, 1, length), F32)]
        + [pltpu.VMEM((heads, length, LANES), F32)]
        + [pltpu.VMEM((heads, length, LANES), BF)] * 2,
        compiler_params=pltpu.CompilerParams(vmem_limit_bytes=VMEM_LIMIT),
    )(drop_counts, lengths, packed, attended, lse, grad_out)


def input_back_kernel(
    gpacked_ref, wcat_ref, normed_ref, tok_ref, gmid_ref, gain_ref,
    ingrad_ref, gqkv_ref, gsum_ref, gbias_ref,
    out_sc, land_sc, send_sem, recv_sem,
):
    group = Group(send_sem, recv_sem)
    rows, width = tok_ref.shape
    chunk = rows // CHUNKS
    scatter = Scatter(group, out_sc, land_sc)
    group.barrier([group.mate, group.peer])

    def terms(member, k):
        start = pl.multiple_of(member * rows + k * chunk, 16)
        return dot_nt(gpacked_ref[pl.ds(start, chunk), :], wcat_ref[...])

    for k in range(CHUNKS):
        scatter.send(0, k, terms(group.far, k))
    for k in range(CHUNKS):
        scatter.send(1, k, terms(group.peer, k) + scatter.arrived(0, k))
    for k in range(CHUNKS):
        scatter.send(2, k, terms(group.mate, k))
    gqkv_ref[...] = dot_tn(normed_ref[...], gpacked_ref[...]).astype(BF)
    gbias_ref[...] = column_sum(gpacked_ref[...].astype(F32))
    sums = [jnp.zeros((1, width), F32)] * 2
    for k in range(CHUNKS):
        part = pl.ds(k * chunk, chunk)
        grad = terms(group.here, k) + scatter.arrived(2, k) + scatter.arrived(1, k)
        unit, inverse = normalize(tok_ref[part, :].astype(F32))
        ingrad_ref[part, :] = gmid_ref[part, :] + normalize_back(
            grad, unit, inverse, gain_ref[...]
        )
        sums = [a + column_sum(b) for a, b in zip(sums, (grad * unit, grad))]
    for i, value in enumerate(sums):
        gsum_ref[i : i + 1, :] = value
    scatter.finish()


def input_back(gpacked, wcat, normed, tokens, gmid, gain):
    rows, width = tokens.shape
    packed_width = gpacked.shape[1]
    return seq_call(
        input_back_kernel, 5, 3 * CHUNKS,
        [pltpu.VMEM((3, rows, width), BF)] * 2,
        (
            jax.ShapeDtypeStruct((rows, width), F32),
            jax.ShapeDtypeStruct((width, packed_width), BF),
            jax.ShapeDtypeStruct((2, width), F32),
            jax.ShapeDtypeStruct((1, packed_width), F32),
        ),
        [VM] * 6,
        name="input_back",
    )(gpacked, wcat, normed, tokens, gmid, gain)


def body(
    cell_tokens, drop_counts, lengths, ln_gain, ln_shift, w_qkv, qv_bias, w_out, out_bias,
    w_up, up_bias, w_down, out_grad,
):
    group = lax.axis_size("seq")
    cells = lax.axis_size("cells")
    place = lax.axis_index("seq")
    unit_rows, part_width = w_up.shape
    _, rows, width = cell_tokens.shape
    share = -(-unit_rows // (group * 8)) * 8
    full = group * share

    gains = ln_gain.astype(F32)
    shifts = ln_shift.astype(F32)
    biases = out_bias.astype(F32)
    tokens = cell_tokens[0]
    head_bias = jnp.concatenate([qv_bias[0], jnp.zeros_like(qv_bias[0]), qv_bias[1]])
    bias_rows = jnp.pad(
        up_bias.astype(F32).reshape(cells, unit_rows), ((0, 0), (0, full - unit_rows))
    ).reshape(cells, group, share)
    bias_unit = lax.dynamic_index_in_dim(bias_rows, place, 1, keepdims=False).reshape(1, -1)

    normed_all, packed, wcat, mine = project(
        tokens, gains[0:1], shifts[0:1], w_qkv, head_bias.astype(F32)[None], w_up, w_down, share
    )
    up_unit = lax.all_gather(mine[0], "cells", axis=0, tiled=True)
    down_unit = lax.all_gather(mine[1], "cells", axis=0, tiled=True)
    attended, lse, cots = attend(packed, out_grad[0], drop_counts, lengths)
    middle, terms, grad_middle, grad_branch, grad_up_unit, grad_down_unit, sums2, gupb = (
        middle_call(
            attended, tokens, cots, w_out, up_unit, down_unit, bias_unit, biases,
            gains[1:2], shifts[1:2],
        )
    )
    branch2 = lax.psum_scatter(terms, "seq", scatter_dimension=0, tiled=True)
    block_out = (middle + (branch2.astype(F32) + biases[1])).astype(BF)
    up_part = lax.psum_scatter(grad_up_unit, "cells", scatter_dimension=0, tiled=True)
    down_part = lax.psum_scatter(grad_down_unit, "cells", scatter_dimension=0, tiled=True)
    unit_bias_grad = gupb.reshape(cells, share)
    placed_bias = lax.dynamic_update_index_in_dim(
        jnp.zeros((cells, group, share), F32), unit_bias_grad, place, 1
    )
    grad_up_bias = placed_bias.reshape(cells, full)[:, :unit_rows].reshape(-1)

    grad_heads, grad_out_own = branch_back(grad_branch, attended, w_out)
    grad_packed = attend_back(packed, attended, lse, grad_heads, drop_counts, lengths)
    in_grad, grad_qkv_own, sums1, gbias = input_back(
        grad_packed, wcat, normed_all, tokens, grad_middle, gains[0:1]
    )

    unit_parts = jnp.stack([up_part, down_part]).reshape(2, share, group, part_width)
    unit_parts = jnp.transpose(unit_parts, (2, 0, 1, 3))
    unit_moved = lax.all_to_all(unit_parts, "seq", split_axis=0, concat_axis=0, tiled=True)
    d_up = unit_moved[:, 0].reshape(full, part_width)[:unit_rows].astype(F32)
    d_down = unit_moved[:, 1].reshape(full, part_width)[:unit_rows].astype(F32)

    grad_qkv_own = jnp.stack(
        [grad_qkv_own[:, t * part_width : (t + 1) * part_width] for t in range(3)]
    )
    d_qkv, d_out = lax.psum((grad_qkv_own, grad_out_own), "cells")
    d_qv_bias = lax.psum(jnp.stack([gbias[0, :part_width], gbias[0, 2 * part_width :]]), "cells")
    d_ln_gain, d_ln_shift, d_out_bias, d_up_bias = lax.psum(
        (
            jnp.stack([sums1[0], sums2[0]]),
            jnp.stack([sums1[1], sums2[1]]),
            sums2[2:4],
            grad_up_bias,
        ),
        ("cells", "seq"),
    )
    return (
        block_out[None], in_grad[None], d_ln_gain, d_ln_shift, d_qkv.astype(F32), d_qv_bias,
        d_out.astype(F32), d_out_bias, d_up, d_up_bias, d_down,
    )


def solution(mesh):
    placed = (
        P("cells", "seq", None), P("cells"), P("cells"), P(), P(), P(None, None, "seq"),
        P(None, "seq"), P("seq", None), P(), P("cells", "seq"), P(), P("cells", "seq"),
        P("cells", "seq", None),
    )
    return jax.shard_map(
        body,
        mesh=mesh,
        in_specs=placed,
        out_specs=(
            P("cells", "seq", None), P("cells", "seq", None), P(), P(), P(None, None, "seq"),
            P(None, "seq"), P("seq", None), P(), P("cells", "seq"), P(), P("cells", "seq"),
        ),
        check_vma=False,
    )
```

time: 764 us -> 574 us (0.75)
  waiting for transfers between devices: 458 us -> 236 us
  Pallas kernels: 50 us -> 219 us
  matrix products: 86.8 us -> 0 us
  other arithmetic: 36.2 us -> 7.95 us
  blocking collectives: 75.5 us -> 60.7 us
    pallas_call x1 -> x5, Pallas kernels: 21.7 us -> 191 us  [the longest x1 74.7 us: middle_call(): seq_call(middle_kernel, 3, 9 * CHUNKS, [pltpu.VMEM((4 * rows, width), BF)...]
    dot_general x12 -> x0, matrix products: 86.8 us -> none  [the longest x3 22.5 us: dot_nt(): lax.dot_general(a, b, (((1,), (1,)), ((), ())), preferred_element_type=F32)]
    all_gather x4 -> x0, waiting for transfers between devices: 84.8 us -> none  [the longest x1 28.8 us: body(): normed_all = lax.all_gather(normed, 'seq', axis=0, tiled=True)]
    reduce_scatter x4 -> x1, waiting for transfers between devices: 113 us -> 30 us  [body(): branch2 = lax.psum_scatter(terms, 'seq', scatter_dimension=0, tiled=True)]
    reduce_scatter x1, waiting for transfers between devices: 24.8 us -> 0.02 us  [body(): lax.psum_scatter(grad_up_unit, 'cells', scatter_dimension=0, tiled=True)]
    reduce_sum x11 -> x0, other arithmetic: 17.8 us -> none  [the longest x3 5.5 us: layer_norm(): return offsets * lax.rsqrt(spread + epsilon) * gain + shift]
    reduce_scatter x1, waiting for transfers between devices: 71.4 us -> 55 us  [body(): lax.psum_scatter(grad_down_unit, 'cells', scatter_dimension=0, tiled=True)]
    all_to_all x1 -> x0, blocking collectives: 15.2 us -> none  [body(): moved = lax.all_to_all(both, 'seq', split_axis=0, concat_axis=0, tiled=True)]
  transfers between devices with their start and end apart: 14 -> 7, of which waited for: 14 -> 5; matrix products, arithmetic and copies ran while one was open for 13% -> 3% of each run, Pallas kernels for 4% -> 19%
where the time goes in v2:
time: 574 us; the launch traced here: 568 us
  waiting for transfers between devices  236 us (41%)
  Pallas kernels  219 us (38%)
  blocking collectives  60.7 us (11%)
  local copies, waits for them, and re-layouts  24.6 us (4%)
  between operations  15.9 us (3%)
  other arithmetic  7.95 us (1%)
    pallas_call x1, Pallas kernels, middle_call(): seq_call(middle_kernel, 3, 9 * CHUNKS, [pltpu.VMEM((4 * rows, width), BF)...  74.7 us
    psum x1, waiting for transfers between devices, body(): d_qkv, d_out = lax.psum((grad_qkv_own, grad_out_own), 'cells')  68.9 us
    all_gather x1, waiting for transfers between devices, body(): down_unit = lax.all_gather(mine[1], 'cells', axis=0, tiled=True)  56.4 us
    reduce_scatter x1, waiting for transfers between devices, body(): lax.psum_scatter(grad_down_unit, 'cells', scatter_dimension=0, tiled=True)  55 us
    psum x1, blocking collectives, body(): lax.psum((jnp.stack([sums1[0], sums2[0]]), jnp.stack([sums1[1], sums2[1]]...  40.2 us
    pallas_call x1, Pallas kernels, project(): seq_call(project_kernel, 1, 3 * CHUNKS + 3, [pltpu.VMEM((4, share, wide),...  34.4 us
    reduce_scatter x1, waiting for transfers between devices, body(): branch2 = lax.psum_scatter(terms, 'seq', scatter_dimension=0, tiled=True)  30 us
    pallas_call x1, Pallas kernels, attend(): seq_call(attend_kernel, 2, 3 * CHUNKS, [pltpu.VMEM((heads, length, LANES)...  28.8 us
  transfers between devices with their start and end apart: 7, of which 5 were waited for; matrix products, arithmetic and copies ran while one was open for 3% of the time, Pallas kernels for 19%

profile of v2, /device:TPU:0, one launch (start us, length us, event | category | flops | bytes accessed | tf_op | source)
XLA Modules:
  0.0 567.8 jit_solution(628095939766177096)
XLA Ops:
  8.0 4.2 copy.39.w_ref
  15.5 34.4 %project.1 = (bf16[1280,1120]{1,0:T(8,128)(2,1)}, bf16[1280,840]{1,0:T(8,128)(2,1)}, bf16[1120,840]{1,0:T(8,128)(2,1)}, bf16[2,144,1120]{2,1,0:T(8,128)(2,1)}) custom-call(bf16[320,1120]{1,0:T(8,128)(2,1)} %bitcast.18, f32[1,1120]{1,0:T(1,128)} %get-tuple-element.111.gain_ref, f32[1,1120]{1,0:T(1,128)} %get-tuple-element.104.shift_ref, ...), custom_call_target="tpu_custom_call" | custom-call | tf_op jit(solution)/shard_map/project/pallas_call | solution.py:239
  49.9 2.0 fusion.4
  55.5 28.8 %attend.1 = (bf16[1280,280]{1,0:T(8,128)(2,1)}, f32[5,1,1280]{2,1,0:T(1,128)}, bf16[1280,1120]{1,0:T(8,128)(2,1)}) custom-call(s32[1]{0:T(128)S(6)} %copy.52.drop_ref, s32[1]{0:T(128)S(6)} %copy.53.len_ref, bf16[1280,840]{1,0:T(8,128)(2,1)} %get-tuple-element.32.packed_ref, bf16[320,1120]{1,0:T(8,128)(2,1)} %bitcast.26), custom_call_target="tpu_custom_call" | custom-call | tf_op jit(solution)/shard_map/attend/pallas_call | solution.py:317
  84.3 23.9 %all-gather.5.cloned.1.call-done = bf16[1,1152,1120]{2,1,0:T(8,128)(2,1)} async-done(((bf16[1,144,1120]{2,1,0:T(8,128)(2,1)}), bf16[1,1152,1120]{2,1,0:T(8,128)(2,1)}) %all-gather.5.cloned.1.call-update) | async-done | bytes 2580496 | tf_op jit(solution)/shard_map/all_gather | solution.py:658
  108.2 56.4 %all-gather.7.cloned.1.call-done = bf16[1,1152,1120]{2,1,0:T(8,128)(2,1)} async-done(((bf16[1,144,1120]{2,1,0:T(8,128)(2,1)}), bf16[1,1152,1120]{2,1,0:T(8,128)(2,1)}) %all-gather.7.cloned.1.call-update) | async-done | bytes 2580496 | tf_op jit(solution)/shard_map/all_gather | solution.py:659
  164.5 74.7 %middle.1 = (f32[320,1120]{1,0:T(8,128)}, bf16[1280,1120]{1,0:T(8,128)(2,1)}, f32[320,1120]{1,0:T(8,128)}, bf16[320,1120]{1,0:T(8,128)(2,1)}, bf16[1152,1120]{1,...) custom-call(bf16[1280,280]{1,0:T(8,128)(2,1)} %get-tuple-element.33.att_ref.out_ref, ...), custom_call_target="tpu_custom_call" | custom-call | tf_op jit(solution)/shard_map/middle/pallas_call | solution.py:439
  239.9 24.2 %branch_back.1 = (bf16[1280,280]{1,0:T(8,128)(2,1)}, bf16[280,1120]{1,0:T(8,128)(2,1)}) custom-call(bf16[320,1120]{1,0:T(8,128)(2,1)} %get-tuple-element.39.gbranch_ref, bf16[1280,280]{1,0:T(8,128)(2,1)} %get-tuple-element.33.att_ref.out_ref, bf16[280,1120]{1,0:T(8,128)(2,1)} %wout_ref.3), custom_call_target="tpu_custom_call" | custom-call | tf_op jit(solution)/shard_map/branch_back/pallas_call | solution.py:491
  264.1 28.0 %attend_back.1.gpacked_ref = bf16[1280,840]{1,0:T(8,128)(2,1)} custom-call(s32[1]{0:T(128)S(6)} %copy.52.drop_ref, s32[1]{0:T(128)S(6)} %copy.53.len_ref, bf16[1280,840]{1,0:T(8,128)(2,1)} %get-tuple-element.32.packed_ref, bf16[1280,280]{1,0:T(8,128)(2,1)} %get-tuple-element.33.att_ref.out_ref, f32[5,1,1280]{2,1,0:T(1,128)} %get-tuple-element.38.lse_ref, ...), custom_call_target="tpu_custom_call" | custom-call | tf_op jit(solution)/shard_map/attend_back/pallas_call | solution.py:565
  292.1 28.7 %input_back.1 = (f32[320,1120]{1,0:T(8,128)}, bf16[1120,840]{1,0:T(8,128)(2,1)}, f32[2,1120]{1,0:T(2,128)}, f32[1,840]{1,0:T(1,128)}) custom-call(bf16[1280,840]{1,0:T(8,128)(2,1)} %attend_back.1.gpacked_ref, bf16[1120,840]{1,0:T(8,128)(2,1)} %get-tuple-element.41.wcat_ref, bf16[1280,1120]{1,0:T(8,128)(2,1)} %get-tuple-element.42.normed_ref, ...), custom_call_target="tpu_custom_call" | custom-call | tf_op jit(solution)/shard_map/input_back/pallas_call | solution.py:619
  320.9 2.7 slice_bitcast_fusion.2
  323.5 2.0 pad_maximum_fusion
  326.5 1.4 stack.37
  327.9 55.0 %reduce-scatter.8.cloned.1.call-done = bf16[144,1120]{1,0:T(8,128)(2,1)} async-done(((bf16[1152,1120]{1,0:T(8,128)(2,1)}), bf16[144,1120]{1,0:T(8,128)(2,1)}) %reduce-scatter.8.cloned.1.call-update) | async-done | bytes 322576 | tf_op jit(solution)/shard_map/reduce_scatter | solution.py:670
  383.0 1.4 stack.38
  385.5 3.5 all-to-all-start
  389.4 20.5 %psum.52 = f32[2,280]{1,0:T(2,128)} all-reduce(f32[2,280]{1,0:T(2,128)S(1)} %pad_maximum_fusion.3), channel_id=1, replica_groups=mesh['cells'=8,'seq'=4] {'cells'}, use_global_device_ids=true, to_apply=%region_4.5 | all-reduce | flops 560 | bytes 4480 | tf_op jit(solution)/shard_map/psum | solution.py:693
  409.9 40.2 %all-reduce.1 = (f32[2,1120]{1,0:T(2,128)}, f32[2,1120]{1,0:T(2,128)}, f32[2,1120]{1,0:T(2,128)}, f32[4480]{0:T(1024)}) all-reduce(f32[2,1120]{1,0:T(2,128)S(1)} %pad_maximum_fusion.1, f32[2,1120]{1,0:T(2,128)S(1)} %pad_maximum_fusion.2, f32[2,1120]{1,0:T(2,128)S(1)} %slice.91, ...), channel_id=1, replica_groups=mesh['cells'=8,'seq'=4] {'cells','seq'}, use_global_device_ids=true, to_apply=%region_1.2 | all-reduce | flops 11200 | bytes 89600 | tf_op jit(solution)/shard_map/psum | solution.py:694
  450.1 68.9 %all-reduce.5.cloned.1.call-done = (bf16[3,1120,280]{2,1,0:T(8,128)(2,1)}, bf16[280,1120]{1,0:T(8,128)(2,1)}) async-done(((bf16[3,1120,280]{2,1,0:T(8,128)(2,1)}, bf16[280,1120]{1,0:T(8,128)(2,1)}), (bf16[3,1120,280]{2,1,0:T(8,128)(2,1)}, bf16[280,1120]{1,0:T(8,128)(2,1)})) %all-reduce.5.cloned.1.call-update) | async-done | bytes 2508816 | tf_op jit(solution)/shard_map/psum | solution.py:692
  519.0 4.6 copy.45
  525.0 1.2 copy.46
  526.2 1.2 copy.47
  527.4 30.0 %reduce-scatter.4.cloned.1.call-done = bf16[320,1120]{1,0:T(8,128)(2,1)} async-done(((bf16[1280,1120]{1,0:T(8,128)(2,1)}), bf16[320,1120]{1,0:T(8,128)(2,1)}) %reduce-scatter.4.cloned.1.call-update) | async-done | bytes 716816 | tf_op jit(solution)/shard_map/reduce_scatter | solution.py:667
  557.3 2.3 fusion
  (77 shorter events, 11.8 us)
Async XLA Ops:
  7.2 5.0 copy-start.3
  7.2 101.0 %all-gather.5.cloned.1.call-start = ((), (), s32[]{:S(2)}) async-start(), calls=%async_computation.7 | async-start | bytes 2985984 | tf_op jit(solution)/shard_map/all_gather | solution.py:658
  8.0 5.1 copy-start.4
  8.0 6.1 %copy-start.7 = (bf16[2,1120]{1,0:T(2,128)(2,1)S(1)}, bf16[2,1120]{1,0:T(2,128)(2,1)}, u32[]{:S(2)}) copy-start(bf16[2,1120]{1,0:T(2,128)(2,1)} %param.17) | copy-start | bytes 13444
  8.0 6.1 %copy-start.8 = (bf16[2,1120]{1,0:T(2,128)(2,1)S(1)}, bf16[2,1120]{1,0:T(2,128)(2,1)}, u32[]{:S(2)}) copy-start(bf16[2,1120]{1,0:T(2,128)(2,1)} %param.16) | copy-start | bytes 13444
  15.4 38.5 %copy-start.9 = (bf16[4480]{0:T(1024)(128)(2,1)S(1)}, bf16[4480]{0:T(1024)(128)(2,1)}, u32[]{:S(2)}) copy-start(bf16[4480]{0:T(1024)(128)(2,1)} %param.23) | copy-start | bytes 26884
  15.5 39.4 %copy-start.11 = (bf16[2,1120]{1,0:T(2,128)(2,1)S(1)}, bf16[2,1120]{1,0:T(2,128)(2,1)}, u32[]{:S(2)}) copy-start(bf16[2,1120]{1,0:T(2,128)(2,1)} %param.21) | copy-start | bytes 13444
  51.9 112.7 %all-gather.7.cloned.1.call-start = ((), (), s32[]{:S(2)}) async-start(), calls=%async_computation.8 | async-start | bytes 2985984 | tf_op jit(solution)/shard_map/all_gather | solution.py:659
  52.6 273.8 %reduce-scatter.6.cloned.1.call-start = ((), (), s32[]{:S(2)}) async-start(), calls=%async_computation.5 | async-start | bytes 2985984 | tf_op jit(solution)/shard_map/reduce_scatter | solution.py:669
  239.3 143.7 %reduce-scatter.8.cloned.1.call-start = ((), (), s32[]{:S(2)}) async-start(), calls=%async_computation.6 | async-start | bytes 2985984 | tf_op jit(solution)/shard_map/reduce_scatter | solution.py:670
  239.8 279.2 %all-reduce.5.cloned.1.call-start = ((), (), s32[]{:S(2)}) async-start(), calls=%async_computation.9 | async-start | bytes 6451200 | tf_op jit(solution)/shard_map/psum | solution.py:692
  325.6 0.7 copy-start.5
  325.6 0.7 copy-start.13
  325.6 0.8 copy-start.10
  325.6 0.8 copy-start.6
  325.6 231.7 %reduce-scatter.4.cloned.1.call-start = ((), (), s32[]{:S(2)}) async-start(), calls=%async_computation.4 | async-start | bytes 3686400 | tf_op jit(solution)/shard_map/reduce_scatter | solution.py:667
  327.9 61.1 %copy-start.12 = (f32[1,1152]{1,0:T(1,128)S(1)}, f32[1,1152]{1,0:T(1,128)}, u32[]{:S(2)}) copy-start(f32[1,1152]{1,0:T(1,128)} %get-tuple-element.52) | copy-start | bytes 13828
  385.5 139.3 %all-to-all-start = ((bf16[4,2,144,280]{3,2,1,0:T(8,128)(2,1)}), bf16[4,2,144,280]{3,2,1,0:T(8,128)(2,1)S(1)}, u32[]{:S(2)}, u32[]{:S(2)}) async-start(bf16[4,2,144,280]{3,2,1,0:T(8,128)(2,1)} %maximum_bitcast_fusion), calls=%async_computation.3 | async-start | bytes 1769472 | tf_op jit(solution)/shard_map/all_to_all | solution.py:685
  519.0 4.6 copy-start.2
  524.9 32.5 %copy-start = (f32[320,1120]{1,0:T(8,128)S(1)}, f32[320,1120]{1,0:T(8,128)}, u32[]{:S(2)}) copy-start(f32[320,1120]{1,0:T(8,128)} %get-tuple-element.36) | copy-start | bytes 4300804
  557.3 2.3 copy-start.1
Sparse Core Ops, SparseCore 0:
  52.0 56.1 all-gather.4
  110.9 53.5 all-gather.6
  239.4 69.5 reduce-scatter.5
  312.9 69.9 reduce-scatter.7
  387.0 131.9 all-reduce.4
  521.4 35.8 reduce-scatter.3
